TPU v7x, 32 devices: a whole 2x2x4 slice. The times are simulated.
32 devices in a mesh: fsdp: 4 (over y, core), ctx: 2 (over x), tp: 4 (over z).
Axes of the slice: x: 2, y: 2, z: 4, core: 2. Of those that a mesh axis runs over, the one named last changes fastest.
Arguments:
- tokens: bfloat16 [4, 1024, 2048], P('fsdp', 'ctx'), may hold values from -6 to 6
- lengths: int32 [4, 3], P('fsdp'), may hold values from 1 to 768, 960 in all within a row
- block_order: int32 [4, 4], P('fsdp'), may hold values from 0 to 3, each once within a row
- ln_gain: bfloat16 [2048], P('fsdp'), may hold values from 0.25 to 1.75
- ln_bias: bfloat16 [2048], P('fsdp'), may hold values from -3 to 3
- qkv_weight: bfloat16 [2048, 3, 2048], P('fsdp', None, 'tp'), may hold values from -0.125 to 0.125
- qkv_bias: bfloat16 [3, 2048], P(None, 'tp'), may hold values from -0.59765625 to 0.59765625
- dense_weight: bfloat16 [2048, 2048], P('fsdp', 'tp'), may hold values from -1 to 1
- dense_bias: bfloat16 [2048], P('fsdp'), may hold values from -3 to 3
- fc1_weight: bfloat16 [2048, 8192], P('fsdp', 'tp'), may hold values from -0.125 to 0.125
- fc1_bias: bfloat16 [8192], P('tp'), may hold values from -3 to 3
- fc2_weight: bfloat16 [2048, 8192], P('fsdp', 'tp'), may hold values from -0.0625 to 0.0625
- fc2_bias: bfloat16 [2048], P('fsdp'), may hold values from -3 to 3
- cotangent: bfloat16 [4, 1024, 2048], P('fsdp', 'ctx'), may hold values from -6 to 6
Outputs:
- output: bfloat16 [4, 1024, 2048], P('fsdp', 'ctx')
- input_grad: float32 [4, 1024, 2048], P('fsdp', 'ctx')
- ln_gain_grad: float32 [2048], P('fsdp')
- ln_bias_grad: float32 [2048], P('fsdp')
- qkv_weight_grad: float32 [2048, 3, 2048], P('fsdp', None, 'tp')
- qkv_bias_grad: float32 [3, 2048], P(None, 'tp')
- dense_weight_grad: float32 [2048, 2048], P('fsdp', 'tp')
- dense_bias_grad: float32 [2048], P('fsdp')
- fc1_weight_grad: float32 [2048, 8192], P('fsdp', 'tp')
- fc1_bias_grad: float32 [8192], P('tp')
- fc2_weight_grad: float32 [2048, 8192], P('fsdp', 'tp')
- fc2_bias_grad: float32 [2048], P('fsdp')
Inputs may be any that keep to these rules, and one draw needn't show every extreme that they name: Each row holds the lengths of 3 sequences packed from the row's start; they sum to 960 and the largest is exactly 768. Each row is a permutation of the 4 block numbers; dealt block j holds packed block block_order[b, j].
All inputs are finite; a program needn't handle non-finite values.
Results may differ from a plain program's by a relative error of at most 0.012.
Values may be sent and summed in bfloat16 or wider, within the bound.
No kernel may reach another device: no remote copies, remote signals or barrier semaphores. Data moves between devices by JAX's collectives and lax.ppermute only.
A program may use at most 256 MiB of HBM per device.

v0:
```python
import math

import jax
import jax.numpy as jnp
from jax import lax
from jax.sharding import PartitionSpec as P

HD = 256
ROT = 64


NORM_EPSILON = 1e-05
MASK_FLOOR = -1000000000.0


def rotation_tables(position):
    frequency = jnp.exp(jnp.arange(ROT // 2, dtype=jnp.float32) * (-2.0 * math.log(10000.0) / ROT))
    angles = position.astype(jnp.float32)[:, None] * frequency[None, :]
    return (jnp.cos(angles)[:, None, :], jnp.sin(angles)[:, None, :])


def rotate(values, cosine_table, sine_table):
    first_half = values[..., : ROT // 2]
    second_half = values[..., ROT // 2 : ROT]
    return jnp.concatenate(
        [
            first_half * cosine_table - second_half * sine_table,
            second_half * cosine_table + first_half * sine_table,
            values[..., ROT:],
        ],
        axis=-1,
    )


def rotate_back(grads, cosine_table, sine_table):
    first_half = grads[..., : ROT // 2]
    second_half = grads[..., ROT // 2 : ROT]
    return jnp.concatenate(
        [
            first_half * cosine_table + second_half * sine_table,
            second_half * cosine_table - first_half * sine_table,
            grads[..., ROT:],
        ],
        axis=-1,
    )


def packed_rows(order_row, first_slot, row_count, block_rows):
    row_index = jnp.arange(row_count, dtype=jnp.int32)
    dealt_slot = first_slot + row_index // block_rows
    selector = dealt_slot[:, None] == jnp.arange(order_row.shape[0], dtype=jnp.int32)[None, :]
    source_block = jnp.sum(jnp.where(selector, order_row[None, :], 0), axis=1, dtype=jnp.int32)
    return source_block * block_rows + row_index % block_rows


def place_rows(packed_at, lengths_row):
    seq_ends = jnp.cumsum(lengths_row, dtype=jnp.int32)
    passed = packed_at[:, None] >= seq_ends[None, :]
    segment = jnp.sum(passed.astype(jnp.int32), axis=1, dtype=jnp.int32)
    before = jnp.sum(jnp.where(passed, lengths_row[None, :], 0), axis=1, dtype=jnp.int32)
    return (segment, packed_at - before)


def gelu_slope(value):
    normal_cdf = 0.5 * (1.0 + lax.erf(value * (1.0 / math.sqrt(2.0))))
    density = jnp.exp(-0.5 * value * value) * (1.0 / math.sqrt(2.0 * math.pi))
    return normal_cdf + value * density


def per_device(
    tokens,
    lengths,
    block_order,
    ln_gain,
    ln_bias,
    qkv_weight,
    qkv_bias,
    dense_weight,
    dense_bias,
    fc1_weight,
    fc1_bias,
    fc2_weight,
    fc2_bias,
    cotangent,
):
    gathered = (
        lax.all_gather(qkv_weight, "fsdp", axis=0, tiled=True),
        lax.all_gather(dense_weight, "fsdp", axis=0, tiled=True),
        lax.all_gather(fc1_weight, "fsdp", axis=0, tiled=True),
        lax.all_gather(fc2_weight, "fsdp", axis=0, tiled=True),
        lax.all_gather(ln_gain, "fsdp", axis=0, tiled=True),
        lax.all_gather(ln_bias, "fsdp", axis=0, tiled=True),
        lax.all_gather(dense_bias, "fsdp", axis=0, tiled=True),
        lax.all_gather(fc2_bias, "fsdp", axis=0, tiled=True),
    )
    qkv_full = gathered[0]
    dense_full = gathered[1]
    fc1_full = gathered[2]
    fc2_full = gathered[3]
    norm_gain = gathered[4].astype(jnp.float32)
    norm_bias = gathered[5].astype(jnp.float32)
    out_bias = gathered[6].astype(jnp.float32) + gathered[7].astype(jnp.float32)
    inputs = tokens[0].astype(jnp.float32)
    row_count = inputs.shape[0]
    block_rows = row_count // 2
    group_rows = row_count * lax.axis_size("ctx")
    lengths_row = lengths[0]
    order_row = block_order[0]
    seq_count = lengths_row.shape[0]
    local_packed = packed_rows(order_row, lax.axis_index("ctx") * 2, row_count, block_rows)
    key_packed = packed_rows(order_row, 0, group_rows, block_rows)
    local_segment, local_position = place_rows(local_packed, lengths_row)
    key_segment = place_rows(key_packed, lengths_row)[0]
    valid_rows = (local_segment < seq_count).astype(jnp.float32)
    allowed = (local_segment[:, None] == key_segment[None, :]) & (
        key_packed[None, :] <= local_packed[:, None]
    )
    cosine_table, sine_table = rotation_tables(local_position)
    score_scale = 1.0 / math.sqrt(HD)
    row_mean = jnp.mean(inputs, axis=1, keepdims=True)
    centred = inputs - row_mean
    variance = jnp.mean(centred * centred, axis=1, keepdims=True)
    inverse = lax.rsqrt(variance + NORM_EPSILON)
    standard = centred * inverse
    normed = (standard * norm_gain + norm_bias).astype(jnp.bfloat16)
    projected = jnp.einsum(
        "td,dce->tce", normed, qkv_full, preferred_element_type=jnp.float32
    ) + qkv_bias.astype(jnp.float32)
    heads_here = projected.shape[2] // HD
    shaped = projected.reshape(row_count, 3, heads_here, HD)
    queries = rotate(shaped[:, 0], cosine_table, sine_table).astype(jnp.bfloat16)
    keys_local = rotate(shaped[:, 1], cosine_table, sine_table).astype(jnp.bfloat16)
    values_local = shaped[:, 2].astype(jnp.bfloat16)
    keys_all, values_all = (
        lax.all_gather(keys_local, "ctx", axis=0, tiled=True),
        lax.all_gather(values_local, "ctx", axis=0, tiled=True),
    )

    def head_scores(head_index):
        scores = (
            jnp.einsum(
                "qe,ke->qk",
                queries[:, head_index],
                keys_all[:, head_index],
                preferred_element_type=jnp.float32,
            )
            * score_scale
        )
        return jnp.where(allowed, scores, MASK_FLOOR)

    head_outputs = []
    log_totals = []
    for head_index in range(heads_here):
        scores = head_scores(head_index)
        row_max = jnp.max(scores, axis=1, keepdims=True)
        exp_scores = jnp.exp(scores - row_max)
        row_total = jnp.sum(exp_scores, axis=1, keepdims=True)
        probabilities = (exp_scores / row_total).astype(jnp.bfloat16)
        head_outputs.append(
            jnp.dot(probabilities, values_all[:, head_index], preferred_element_type=jnp.float32)
        )
        log_totals.append(row_max + jnp.log(row_total))
    attended = (
        (jnp.stack(head_outputs, axis=1) * valid_rows[:, None, None])
        .astype(jnp.bfloat16)
        .reshape(row_count, heads_here * HD)
    )
    pre_act = jnp.dot(normed, fc1_full, preferred_element_type=jnp.float32) + fc1_bias.astype(
        jnp.float32
    )
    hidden = jax.nn.gelu(pre_act, approximate=False).astype(jnp.bfloat16)
    partial_out = jnp.einsum(
        "te,de->td", attended, dense_full, preferred_element_type=jnp.float32
    ) + jnp.einsum("tf,df->td", hidden, fc2_full, preferred_element_type=jnp.float32)
    summed = lax.psum(partial_out, "tp")
    output = (inputs + summed + out_bias).astype(jnp.bfloat16)
    upstream_low = cotangent[0]
    upstream = upstream_low.astype(jnp.float32)
    out_bias_grad = jnp.sum(upstream, axis=0)
    dense_grad = jnp.einsum("td,te->de", upstream_low, attended, preferred_element_type=jnp.float32)
    fc2_grad = jnp.einsum("td,tf->df", upstream_low, hidden, preferred_element_type=jnp.float32)
    attended_grad = (
        jnp.dot(upstream_low, dense_full, preferred_element_type=jnp.float32).astype(jnp.bfloat16)
        * valid_rows[:, None].astype(jnp.bfloat16)
    ).reshape(row_count, heads_here, HD)
    hidden_grad = jnp.dot(upstream_low, fc2_full, preferred_element_type=jnp.float32)
    pre_grad = (hidden_grad * gelu_slope(pre_act)).astype(jnp.bfloat16)
    fc1_bias_grad = jnp.sum(pre_grad.astype(jnp.float32), axis=0)
    fc1_grad = jnp.einsum("td,tf->df", normed, pre_grad, preferred_element_type=jnp.float32)
    normed_grad = jnp.einsum("tf,df->td", pre_grad, fc1_full, preferred_element_type=jnp.float32)
    query_pieces = []
    key_pieces = []
    value_pieces = []
    for head_index in range(heads_here):
        probs_full = jnp.exp(head_scores(head_index) - log_totals[head_index])
        probs_low = probs_full.astype(jnp.bfloat16)
        head_grad = attended_grad[:, head_index]
        prob_grad = jnp.einsum(
            "qe,ke->qk", head_grad, values_all[:, head_index], preferred_element_type=jnp.float32
        )
        row_delta = jnp.sum(probs_full * prob_grad, axis=1, keepdims=True)
        score_grad = (probs_full * (prob_grad - row_delta)).astype(jnp.bfloat16)
        query_pieces.append(
            jnp.dot(score_grad, keys_all[:, head_index], preferred_element_type=jnp.float32)
            * score_scale
        )
        key_pieces.append(
            jnp.einsum(
                "qk,qe->ke", score_grad, queries[:, head_index], preferred_element_type=jnp.float32
            )
            * score_scale
        )
        value_pieces.append(
            jnp.einsum("qk,qe->ke", probs_low, head_grad, preferred_element_type=jnp.float32)
        )
    own_keys, own_values = (
        lax.psum_scatter(jnp.stack(key_pieces, axis=1), "ctx", scatter_dimension=0, tiled=True),
        lax.psum_scatter(jnp.stack(value_pieces, axis=1), "ctx", scatter_dimension=0, tiled=True),
    )
    query_turned = rotate_back(jnp.stack(query_pieces, axis=1), cosine_table, sine_table)
    key_turned = rotate_back(own_keys, cosine_table, sine_table)
    proj_grad = (
        jnp.stack([query_turned, key_turned, own_values], axis=1)
        .astype(jnp.bfloat16)
        .reshape(row_count, 3, heads_here * HD)
    )
    qkv_bias_grad = jnp.sum(proj_grad.astype(jnp.float32), axis=0)
    qkv_grad = jnp.einsum("td,tce->dce", normed, proj_grad, preferred_element_type=jnp.float32)
    normed_grad = normed_grad + jnp.einsum(
        "tce,dce->td", proj_grad, qkv_full, preferred_element_type=jnp.float32
    )
    full_grad = lax.psum(normed_grad, "tp")
    gain_grad = jnp.sum(full_grad * standard, axis=0)
    shift_grad = jnp.sum(full_grad, axis=0)
    scaled = full_grad * norm_gain
    input_grad = upstream + inverse * (
        scaled
        - jnp.mean(scaled, axis=1, keepdims=True)
        - standard * jnp.mean(scaled * standard, axis=1, keepdims=True)
    )
    bias_sums = lax.psum((qkv_bias_grad, fc1_bias_grad), ("fsdp", "ctx"))
    reduced = (
        lax.psum_scatter(qkv_grad, ("fsdp", "ctx"), scatter_dimension=0, tiled=True),
        lax.psum_scatter(dense_grad, ("fsdp", "ctx"), scatter_dimension=0, tiled=True),
        lax.psum_scatter(fc1_grad, ("fsdp", "ctx"), scatter_dimension=0, tiled=True),
        lax.psum_scatter(fc2_grad, ("fsdp", "ctx"), scatter_dimension=0, tiled=True),
        lax.psum_scatter(gain_grad, ("fsdp", "ctx"), scatter_dimension=0, tiled=True),
        lax.psum_scatter(shift_grad, ("fsdp", "ctx"), scatter_dimension=0, tiled=True),
        lax.psum_scatter(out_bias_grad, ("fsdp", "ctx"), scatter_dimension=0, tiled=True),
    )
    shards = (
        lax.all_gather(reduced[0], "ctx", axis=0, tiled=True),
        lax.all_gather(reduced[1], "ctx", axis=0, tiled=True),
        lax.all_gather(reduced[2], "ctx", axis=0, tiled=True),
        lax.all_gather(reduced[3], "ctx", axis=0, tiled=True),
        lax.all_gather(reduced[4], "ctx", axis=0, tiled=True),
        lax.all_gather(reduced[5], "ctx", axis=0, tiled=True),
        lax.all_gather(reduced[6], "ctx", axis=0, tiled=True),
    )
    return (
        output[None],
        input_grad[None],
        shards[4],
        shards[5],
        shards[0],
        bias_sums[0],
        shards[1],
        shards[6],
        shards[2],
        bias_sums[1],
        shards[3],
        shards[6],
    )


def solution(mesh):
    placed = (
        P("fsdp", "ctx", None),
        P("fsdp", None),
        P("fsdp", None),
        P("fsdp"),
        P("fsdp"),
        P("fsdp", None, "tp"),
        P(None, "tp"),
        P("fsdp", "tp"),
        P("fsdp"),
        P("fsdp", "tp"),
        P("tp"),
        P("fsdp", "tp"),
        P("fsdp"),
        P("fsdp", "ctx", None),
    )
    return jax.shard_map(
        per_device,
        mesh=mesh,
        in_specs=placed,
        out_specs=(
            P("fsdp", "ctx", None),
            P("fsdp", "ctx", None),
            P("fsdp"),
            P("fsdp"),
            P("fsdp", None, "tp"),
            P(None, "tp"),
            P("fsdp", "tp"),
            P("fsdp"),
            P("fsdp", "tp"),
            P("tp"),
            P("fsdp", "tp"),
            P("fsdp"),
        ),
        check_vma=False,
    )
```

profile of v0, /device:TPU:0, one launch (start us, length us, event | category | flops | bytes accessed | tf_op | source)
XLA Modules:
  0.0 1210.3 jit_solution(16124537954326559841)
XLA Ops:
  7.3 2.7 copy.57
  11.0 6.2 all-gather.2
  17.2 5.5 all-gather.1
  24.5 34.9 %all-gather.19.cloned.1.call-done = bf16[2048,3,512]{0,2,1:T(8,128)(2,1)} async-done(((bf16[512,3,512]{0,2,1:T(8,128)(2,1)}), bf16[2048,3,512]{0,2,1:T(8,128)(2,1)}) %all-gather.19.cloned.1.call-update) | async-done | bytes 6291472 | tf_op jit(solution)/shard_map/all_gather | solution.py:87
  59.3 5.9 fusion.46
  65.6 1.0 subtract_convert_fusion.3
  69.2 14.3 %all-gather.23.cloned.1.call-done = bf16[2048,512]{1,0:T(8,128)(2,1)} async-done(((bf16[512,512]{1,0:T(8,128)(2,1)}), bf16[2048,512]{1,0:T(8,128)(2,1)}) %all-gather.23.cloned.1.call-update) | async-done | bytes 2097168 | tf_op jit(solution)/shard_map/all_gather | solution.py:88
  83.5 4.3 fusion.58
  87.8 2.1 slice.201
  90.0 0.9 pad_maximum_fusion.5
  90.9 16.0 %all-gather.21.cloned.1.call-done = bf16[1024,2,256]{0,2,1:T(8,128)(2,1)} async-done(((bf16[512,2,256]{0,2,1:T(8,128)(2,1)}), bf16[1024,2,256]{0,2,1:T(8,128)(2,1)}) %all-gather.21.cloned.1.call-update) | async-done | bytes 1048592 | tf_op jit(solution)/shard_map/all_gather | solution.py:135
  106.9 1.9 fusion.97
  109.4 1.6 fusion.98
  112.8 1.5 pad_maximum_fusion.1
  114.8 15.4 %all-gather.37.cloned.1.call-done = bf16[1024,1,2,256]{0,3,2,1:T(8,128)(2,1)} async-done(((bf16[512,1,2,256]{0,3,2,1:T(8,128)(2,1)}), bf16[1024,1,2,256]{0,3,2,1:T(8,128)(2,1)}) %all-gather.37.cloned.1.call-update) | async-done | bytes 1048592 | tf_op jit(solution)/shard_map/all_gather | solution.py:136
  130.2 2.5 multiply_reduce_fusion.2
  137.1 1.5 pad_maximum_fusion
  140.1 2.4 convolution_bitcast_fusion.4
  144.2 3.3 convolution_bitcast_fusion.1
  147.5 1.9 fusion.57
  149.4 2.0 fusion.56
  152.3 12.5 %reduce-scatter.9.cloned.1.call-done = f32[512,2,256]{2,0,1:T(8,128)} async-done(((f32[1024,2,256]{2,0,1:T(8,128)}), f32[512,2,256]{2,0,1:T(8,128)}) %reduce-scatter.9.cloned.1.call-update) | async-done | bytes 1048592 | tf_op jit(solution)/shard_map/reduce_scatter | solution.py:218
  164.9 2.1 convert.64
  166.9 2.0 copy.60
  169.0 2.1 copy.63
  171.0 28.4 %reduce-scatter.7.cloned.1.call-done = f32[512,2,256]{0,2,1:T(8,128)} async-done(((f32[1024,2,256]{0,2,1:T(8,128)}), f32[512,2,256]{0,2,1:T(8,128)}) %reduce-scatter.7.cloned.1.call-update) | async-done | bytes 1048592 | tf_op jit(solution)/shard_map/reduce_scatter | solution.py:217
  199.5 1.2 slice.202
  200.7 1.4 add_convert_fusion.1
  202.0 1.0 pad_maximum_fusion.7
  203.1 2.1 copy.61
  205.1 2.1 copy.62
  207.2 8.8 fusion.40
  216.7 42.6 %all-gather.25.cloned.1.call-done = bf16[2048,2048]{1,0:T(8,128)(2,1)} async-done(((bf16[512,2048]{1,0:T(8,128)(2,1)}), bf16[2048,2048]{1,0:T(8,128)(2,1)}) %all-gather.25.cloned.1.call-update) | async-done | bytes 8388624 | tf_op jit(solution)/shard_map/all_gather | solution.py:89
  259.3 17.2 %fusion.20 = (bf16[512,2048]{1,0:T(8,128)(2,1)}, f32[512,2048]{1,0:T(8,128)}) fusion(f32[2048]{0:T(1024)S(1)} %convert_element_type.135, bf16[2048,2048]{1,0:T(8,128)(2,1)} %all-gather.25.cloned.1.call-done, bf16[1,512,2048]{2,1,0:T(8,128)(2,1)S(1)} %copy-done, f32[2048]{0:T(1024)S(1)} %bitcast.223, f32[2048]{0:T(1024)S(1)} %bitcast.214, ...), kind=kOutput, calls=%fused_computation.27 | convolution fusion | flops 4370464768 | bytes 16805888 | tf_op jit(solution)/shard_map/dot_general | solution.py:168
  276.5 42.7 %all-gather.27.cloned.1.call-done = bf16[2048,2048]{1,0:T(8,128)(2,1)} async-done(((bf16[512,2048]{1,0:T(8,128)(2,1)}), bf16[2048,2048]{1,0:T(8,128)(2,1)}) %all-gather.27.cloned.1.call-update) | async-done | bytes 8388624 | tf_op jit(solution)/shard_map/all_gather | solution.py:90
  319.2 9.4 convert_reduce_fusion.2
  328.6 1.3 copy-done.41
  329.9 8.8 fusion.92
  339.0 12.5 %convolution_bitcast_fusion = f32[2048,2048]{0,1:T(8,128)} fusion(bf16[512,2048]{1,0:T(8,128)(2,1)} %get-tuple-element.96, bf16[1,512,2048]{2,1,0:T(8,128)(2,1)} %param.27), kind=kOutput, calls=%fused_computation | convolution fusion | flops 4294967296 | bytes 20971520 | tf_op jit(solution)/shard_map/td,tf->df/dot_general | solution.py:181
  352.2 0.9 fusion.63
  353.1 10.8 fusion.99
  363.9 9.8 fusion.100
  374.6 6.5 convolution_add_fusion
  381.1 8.8 bitcast_add_fusion
  390.0 79.6 %reduce-scatter.11.cloned.1.call-done = f32[256,3,512]{2,0,1:T(8,128)} async-done(((f32[2048,3,512]{2,0,1:T(8,128)}), f32[256,3,512]{2,0,1:T(8,128)}) %reduce-scatter.11.cloned.1.call-update) | async-done | bytes 1572880 | tf_op jit(solution)/shard_map/reduce_scatter | solution.py:243
  469.7 119.7 %reduce-scatter.15.cloned.1.call-done = f32[256,2048]{1,0:T(8,128)} async-done(((f32[2048,2048]{1,0:T(8,128)}), f32[256,2048]{1,0:T(8,128)}) %reduce-scatter.15.cloned.1.call-update) | async-done | bytes 2097168 | tf_op jit(solution)/shard_map/reduce_scatter | solution.py:245
  589.5 119.4 %reduce-scatter.17.cloned.1.call-done = f32[256,2048]{0,1:T(8,128)} async-done(((f32[2048,2048]{0,1:T(8,128)}), f32[256,2048]{0,1:T(8,128)}) %reduce-scatter.17.cloned.1.call-update) | async-done | bytes 2097168 | tf_op jit(solution)/shard_map/reduce_scatter | solution.py:246
  710.2 5.2 all-gather.4
  715.4 5.2 all-gather.3
  720.6 1.3 convert_reduce_fusion.3
  721.9 9.9 all-gather.31.cloned.1.call-done
  731.7 2.5 copy.66
  734.3 291.4 %all-reduce.7.cloned.1.call-done = (f32[512,2048]{1,0:T(8,128)}, f32[512,2048]{1,0:T(8,128)}) async-done(((f32[512,2048]{1,0:T(8,128)}, f32[512,2048]{1,0:T(8,128)}), (f32[512,2048]{1,0:T(8,128)}, f32[512,2048]{1,0:T(8,128)})) %all-reduce.7.cloned.1.call-update) | async-done | bytes 8388624 | tf_op jit(solution)/shard_map/psum | solution.py:175
  1025.6 3.9 fusion.13
  1029.8 6.1 convert_reduce_fusion
  1035.8 28.5 %all-reduce.3 = (f32[2048]{0:T(1024)S(1)}, f32[2048]{0:T(1024)S(1)}, f32[3,512]{1,0:T(4,128)}, f32[2048]{0:T(1024)S(1)}, f32[2048]{0:T(1024)}) all-reduce(f32[2048]{0:T(1024)S(1)} %get-tuple-element.60, f32[2048]{0:T(1024)S(1)} %get-tuple-element.63, ...), channel_id=5, replica_groups=mesh['fsdp'=4,'ctx'=2,'tp'=4] {'fsdp','ctx'}, use_global_device_ids=true, to_apply=%region_21.22.clone | all-reduce | flops 9728 | bytes 77824
  1064.4 4.4 all-gather.7
  1068.8 4.3 all-gather.5
  1073.2 4.2 all-gather.6
  1077.5 54.2 %all-gather.33.cloned.1.call-done = f32[512,2048]{1,0:T(8,128)} async-done(((f32[256,2048]{1,0:T(8,128)}), f32[512,2048]{1,0:T(8,128)}) %all-gather.33.cloned.1.call-update) | async-done | bytes 4194320 | tf_op jit(solution)/shard_map/all_gather | solution.py:254
  1131.6 58.1 %all-gather.35.cloned.1.call-done = f32[512,2048]{0,1:T(8,128)} async-done(((f32[256,2048]{0,1:T(8,128)}), f32[512,2048]{0,1:T(8,128)}) %all-gather.35.cloned.1.call-update) | async-done | bytes 4194320 | tf_op jit(solution)/shard_map/all_gather | solution.py:255
  1189.8 5.3 copy.67
  1196.8 3.9 copy.84
  1201.3 2.0 copy.86
  (175 shorter events, 22.8 us)
Async XLA Ops:
  7.2 3.7 copy-start.32
  7.2 3.8 copy-start.33
  7.2 3.8 copy-start.34
  7.2 15.5 %copy-start.30 = (bf16[3,512]{1,0:T(4,128)(2,1)S(1)}, bf16[3,512]{1,0:T(4,128)(2,1)}, u32[]{:S(2)}) copy-start(bf16[3,512]{1,0:T(4,128)(2,1)} %param.20) | copy-start | bytes 9220
  7.2 15.5 %copy-start.37 = (s32[1,3]{1,0:T(1,128)S(1)}, s32[1,3]{1,0:T(1,128)}, u32[]{:S(2)}) copy-start(s32[1,3]{1,0:T(1,128)} %param.15) | copy-start | bytes 40
  7.2 15.8 %copy-start = (bf16[1,512,2048]{2,1,0:T(8,128)(2,1)S(1)}, bf16[1,512,2048]{2,1,0:T(8,128)(2,1)}, u32[]{:S(2)}) copy-start(bf16[1,512,2048]{2,1,0:T(8,128)(2,1)} %param.14) | copy-start | bytes 6291460
  7.2 52.1 %all-gather.19.cloned.1.call-start = ((), (), s32[]{:S(2)}) async-start(), calls=%async_computation.6 | async-start | bytes 7864320 | tf_op jit(solution)/shard_map/all_gather | solution.py:87
  10.0 73.5 %all-gather.23.cloned.1.call-start = ((), (), s32[]{:S(2)}) async-start(), calls=%async_computation.8 | async-start | bytes 2621440 | tf_op jit(solution)/shard_map/all_gather | solution.py:88
  10.8 96.1 %all-gather.21.cloned.1.call-start = ((), (), s32[]{:S(2)}) async-start(), calls=%async_computation.7 | async-start | bytes 1572864 | tf_op jit(solution)/shard_map/all_gather | solution.py:135
  11.0 12.1 copy-start.26
  17.2 48.0 %copy-start.28 = (f32[4,1,512]{2,1,0:T(1,128)}, f32[4,1,512]{2,1,0:T(1,128)S(1)}, u32[]{:S(2)}) copy-start(f32[4,1,512]{2,1,0:T(1,128)S(1)} %convert_element_type.153) | copy-start | bytes 24580
  23.0 45.6 %copy-start.27 = (s32[512]{0:T(512)}, s32[512]{0:T(512)S(1)}, u32[]{:S(2)}) copy-start(s32[512]{0:T(512)S(1)} %get-tuple-element.65) | copy-start | bytes 6148
  24.5 41.1 %copy-start.21 = (f32[512,32]{0,1:T(8,128)}, f32[512,32]{0,1:T(8,128)S(1)}, u32[]{:S(2)}) copy-start(f32[512,32]{0,1:T(8,128)S(1)} %get-tuple-element.92) | copy-start | bytes 196612
  24.5 41.1 %copy-start.22 = (f32[512,32]{0,1:T(8,128)}, f32[512,32]{0,1:T(8,128)S(1)}, u32[]{:S(2)}) copy-start(f32[512,32]{0,1:T(8,128)S(1)} %get-tuple-element.93) | copy-start | bytes 196612
  65.3 1.7 copy-start.12
  67.8 62.4 %all-gather.37.cloned.1.call-start = ((), (), s32[]{:S(2)}) async-start(), calls=%async_computation.21 | async-start | bytes 1572864 | tf_op jit(solution)/shard_map/all_gather | solution.py:136
  68.0 19.8 %copy-start.25 = (s32[1024]{0:T(1024)}, s32[1024]{0:T(1024)S(1)}, u32[]{:S(2)}) copy-start(s32[1024]{0:T(1024)S(1)} %fusion.79) | copy-start | bytes 12292
  90.0 74.9 %reduce-scatter.9.cloned.1.call-start = ((), (), s32[]{:S(2)}) async-start(), calls=%async_computation.12 | async-start | bytes 3145728 | tf_op jit(solution)/shard_map/reduce_scatter | solution.py:218
  106.9 2.4 copy-start.38
  108.8 2.7 copy-start.1
  108.8 2.7 copy-start.13
  111.0 1.8 copy-start.3
  114.3 85.2 %reduce-scatter.7.cloned.1.call-start = ((), (), s32[]{:S(2)}) async-start(), calls=%async_computation.11 | async-start | bytes 3145728 | tf_op jit(solution)/shard_map/reduce_scatter | solution.py:217
  130.2 2.5 copy-start.4
  132.7 1.9 copy-start.2
  132.7 2.2 copy-start.19
  133.3 2.9 copy-start.10
  136.1 1.0 copy-start.11
  138.5 1.6 copy-start.20
  138.6 120.8 %all-gather.25.cloned.1.call-start = ((), (), s32[]{:S(2)}) async-start(), calls=%async_computation.9 | async-start | bytes 10485760 | tf_op jit(solution)/shard_map/all_gather | solution.py:89
  139.3 179.9 %all-gather.27.cloned.1.call-start = ((), (), s32[]{:S(2)}) async-start(), calls=%async_computation.10 | async-start | bytes 10485760 | tf_op jit(solution)/shard_map/all_gather | solution.py:90
  140.1 234.2 %reduce-scatter.13.cloned.1.call-start = ((), (), s32[]{:S(2)}) async-start(), calls=%async_computation.15 | async-start | bytes 4718592 | tf_op jit(solution)/shard_map/reduce_scatter | solution.py:244
  140.1 2.4 copy-start.5
  142.5 0.7 copy-start.23
  142.6 1.6 copy-start.7
  147.5 322.2 %reduce-scatter.11.cloned.1.call-start = ((), (), s32[]{:S(2)}) async-start(), calls=%async_computation.13 | async-start | bytes 14155776 | tf_op jit(solution)/shard_map/reduce_scatter | solution.py:243
  149.4 2.0 copy-start.17
  151.5 0.8 copy-start.18
  216.0 0.7 copy-start.31
  216.0 43.3 %copy-start.29 = (f32[4,1,512]{2,1,0:T(1,128)S(1)}, f32[4,1,512]{2,1,0:T(1,128)}, u32[]{:S(2)}) copy-start(f32[4,1,512]{2,1,0:T(1,128)} %copy-done.28) | copy-start | bytes 24580
  216.0 373.4 %reduce-scatter.15.cloned.1.call-start = ((), (), s32[]{:S(2)}) async-start(), calls=%async_computation.17 | async-start | bytes 18874368 | tf_op jit(solution)/shard_map/reduce_scatter | solution.py:245
  328.6 1.3 copy-start.41
  338.7 370.1 %reduce-scatter.17.cloned.1.call-start = ((), (), s32[]{:S(2)}) async-start(), calls=%async_computation.19 | async-start | bytes 18874368 | tf_op jit(solution)/shard_map/reduce_scatter | solution.py:246
  351.5 0.7 copy-start.24
  351.6 380.2 %all-gather.31.cloned.1.call-start = ((), (), s32[]{:S(2)}) async-start(), calls=%async_computation.16 | async-start | bytes 1572864 | tf_op jit(solution)/shard_map/all_gather | solution.py:253
  353.1 10.8 copy-start.42
  374.3 6.8 copy-start.14
  374.3 6.8 copy-start.15
  374.3 651.4 %all-reduce.7.cloned.1.call-start = ((), (), s32[]{:S(2)}) async-start(), calls=%async_computation.22 | async-start | bytes 16777216 | tf_op jit(solution)/shard_map/psum | solution.py:175
  374.6 6.5 copy-start.16
  374.6 6.5 copy-start.40
  389.9 319.0 %copy-start.35 = (bf16[512]{0:T(512)(128)(2,1)S(1)}, bf16[512]{0:T(512)(128)(2,1)}, u32[]{:S(2)}) copy-start(bf16[512]{0:T(512)(128)(2,1)} %param.22) | copy-start | bytes 3076
  389.9 319.0 %copy-start.36 = (bf16[512]{0:T(512)(128)(2,1)S(1)}, bf16[512]{0:T(512)(128)(2,1)}, u32[]{:S(2)}) copy-start(bf16[512]{0:T(512)(128)(2,1)} %param.26) | copy-start | bytes 3076
  389.9 319.0 %copy-start.39 = (u32[32]{0:T(128)S(1)}, u32[32]{0:T(128)}, u32[]{:S(2)}) copy-start(u32[32]{0:T(128)} %constant.160) | copy-start | bytes 388
  390.0 687.5 %all-gather.29.cloned.1.call-start = ((), (), s32[]{:S(2)}) async-start(), calls=%async_computation.14 | async-start | bytes 4718592 | tf_op jit(solution)/shard_map/all_gather | solution.py:252
  469.7 661.9 %all-gather.33.cloned.1.call-start = ((), (), s32[]{:S(2)}) async-start(), calls=%async_computation.18 | async-start | bytes 6291456 | tf_op jit(solution)/shard_map/all_gather | solution.py:254
  589.5 600.3 %all-gather.35.cloned.1.call-start = ((), (), s32[]{:S(2)}) async-start(), calls=%async_computation.20 | async-start | bytes 6291456 | tf_op jit(solution)/shard_map/all_gather | solution.py:255
  1025.6 3.9 copy-start.6
  1025.6 4.1 copy-start.8
  1195.1 6.2 copy-start.9
Sparse Core Ops, SparseCore 0:
  10.2 49.1 all-gather.18
  60.9 22.5 all-gather.22
  85.6 21.2 all-gather.20
  108.9 21.2 all-gather.36
  132.9 31.9 reduce-scatter.8
  167.5 31.8 reduce-scatter.6
  201.0 58.2 all-gather.24
  260.9 58.2 all-gather.26
  323.1 51.0 reduce-scatter.12
  377.6 92.0 reduce-scatter.10
  473.2 116.1 reduce-scatter.14
  592.9 115.9 reduce-scatter.16
  710.4 21.2 all-gather.30
  734.8 290.8 all-reduce.6
  1027.0 46.3 all-gather.28
  1074.8 56.7 all-gather.32
  1133.0 56.7 all-gather.34
where the time goes:
time: 1220 us; the launch traced here: 1210 us
  waiting for transfers between devices  942 us (77%)
  matrix products  122 us (10%)
  blocking collectives  63.4 us (5%)
  local copies, waits for them, and re-layouts  37.8 us (3%)
  other arithmetic  27.6 us (2%)
  between operations  15.8 us (1%)
    psum x1, waiting for transfers between devices, per_device(): summed = lax.psum(partial_out, 'tp')  291 us
    reduce_scatter x1, waiting for transfers between devices, per_device(): lax.psum_scatter(fc1_grad, ('fsdp', 'ctx'), scatter_dimension=0, tiled=True)  120 us
    reduce_scatter x1, waiting for transfers between devices, per_device(): lax.psum_scatter(fc2_grad, ('fsdp', 'ctx'), scatter_dimension=0, tiled=True)  119 us
    reduce_scatter x1, waiting for transfers between devices, per_device(): lax.psum_scatter(qkv_grad, ('fsdp', 'ctx'), scatter_dimension=0, tiled=True)  79.6 us
    all_gather x1, waiting for transfers between devices, per_device(): lax.all_gather(reduced[3], 'ctx', axis=0, tiled=True)  58.1 us
    all_gather x1, waiting for transfers between devices, per_device(): lax.all_gather(reduced[2], 'ctx', axis=0, tiled=True)  54.2 us
    all_gather x1, waiting for transfers between devices, per_device(): lax.all_gather(fc2_weight, 'fsdp', axis=0, tiled=True)  42.7 us
    all_gather x1, waiting for transfers between devices, per_device(): lax.all_gather(fc1_weight, 'fsdp', axis=0, tiled=True)  42.6 us
  transfers between devices with their start and end apart: 17, of which 16 were waited for; matrix products, arithmetic and copies ran while one was open for 14% of the time, Pallas kernels for 0%

commit v1 on v0

v1 whole, which is shorter than its diff:
```python
import math

import jax
import jax.numpy as jnp
from jax import lax
from jax.sharding import PartitionSpec as P

HD = 256
ROT = 64


NORM_EPSILON = 1e-05
MASK_FLOOR = -1000000000.0
F32 = jnp.float32
BF16 = jnp.bfloat16


def rotation_tables(position):
    frequency = jnp.exp(jnp.arange(ROT // 2, dtype=F32) * (-2.0 * math.log(10000.0) / ROT))
    angles = position.astype(F32)[:, None] * frequency[None, :]
    return (jnp.cos(angles), jnp.sin(angles))


def rotate(values, cosine_table, sine_table):
    first_half = values[..., : ROT // 2]
    second_half = values[..., ROT // 2 : ROT]
    return jnp.concatenate(
        [
            first_half * cosine_table - second_half * sine_table,
            second_half * cosine_table + first_half * sine_table,
            values[..., ROT:],
        ],
        axis=-1,
    )


def rotate_back(grads, cosine_table, sine_table):
    return rotate(grads, cosine_table, -sine_table)


def packed_rows(order_row, slots, block_rows):
    selector = slots[:, None] == jnp.arange(order_row.shape[0], dtype=jnp.int32)[None, :]
    source_block = jnp.sum(jnp.where(selector, order_row[None, :], 0), axis=1, dtype=jnp.int32)
    within = jnp.arange(block_rows, dtype=jnp.int32)
    return (source_block[:, None] * block_rows + within[None, :]).reshape(-1)


def place_rows(packed_at, lengths_row):
    seq_ends = jnp.cumsum(lengths_row, dtype=jnp.int32)
    passed = packed_at[:, None] >= seq_ends[None, :]
    segment = jnp.sum(passed.astype(jnp.int32), axis=1, dtype=jnp.int32)
    before = jnp.sum(jnp.where(passed, lengths_row[None, :], 0), axis=1, dtype=jnp.int32)
    return (segment, packed_at - before)


def dot(a, b, contract):
    return lax.dot_general(a, b, (contract, ((), ())), preferred_element_type=F32)


def swap(x, bit):
    size = lax.axis_size("fsdp")
    return lax.ppermute(x, "fsdp", [(i, i ^ bit) for i in range(size)])


def ctx_pair(x):
    return lax.ppermute(x, "ctx", [(0, 1), (1, 0)])


def ctx_sum(x):
    if lax.axis_size("ctx") == 2:
        return x.astype(F32) + ctx_pair(x).astype(F32)
    return lax.psum(x.astype(F32), "ctx")


def tp_shift(x, d):
    size = lax.axis_size("tp")
    return lax.ppermute(x, "tp", [(i, (i + d) % size) for i in range(size)])


def blocks(x, order):
    width = x.shape[1] // 4
    return jnp.concatenate([x[:, k * width : (k + 1) * width] for k in order], axis=1)


def framed(x, me):
    width = x.shape[1] // 4
    return jnp.concatenate(
        [lax.dynamic_slice_in_dim(x, (me ^ k) * width, width, axis=1) for k in range(4)], axis=1
    )


def half_of(x, which, axis):
    size = x.shape[axis] // 2
    return lax.dynamic_slice_in_dim(x, which * size, size, axis=axis)


def in_order(mine, other, core, axis):
    return jnp.where(
        core == 0,
        jnp.concatenate([mine, other], axis=axis),
        jnp.concatenate([other, mine], axis=axis),
    )


def gather_weight(mine, other):
    return jnp.concatenate([mine, swap(other, 1), swap(mine, 2), swap(other, 3)], axis=0)


def reduce_weight(left, right):
    rows = left.shape[1] // 2
    far = dot(left[:, rows:], right, ((0,), (0,))).astype(BF16)
    near = (dot(left[:, :rows], right, ((0,), (0,))) + swap(far, 2).astype(F32)).astype(BF16)
    kept, given = near[: rows // 2], near[rows // 2 :]
    return ctx_sum(kept), ctx_sum(swap(given, 1))


def scatter_rows(own, tp_index):
    size = lax.axis_size("tp")
    rows = own.shape[0] // size

    def part(d):
        return lax.dynamic_slice_in_dim(own, ((tp_index + d) % size) * rows, rows, axis=0)

    total = part(0)
    for d in range(1, size):
        total = total + tp_shift(part(d).astype(BF16), d).astype(F32)
    return total


def gather_rows(part, tp_index, dtype):
    size = lax.axis_size("tp")
    rows = part.shape[0]
    whole = jnp.zeros((rows * size, part.shape[1]), dtype)
    for d in range(size):
        piece = tp_shift(part, d) if d else part
        at = ((tp_index - d) % size) * rows
        whole = lax.dynamic_update_slice_in_dim(whole, piece.astype(dtype), at, axis=0)
    return whole


def per_device(
    tokens,
    lengths,
    block_order,
    ln_gain,
    ln_bias,
    qkv_weight,
    qkv_bias,
    dense_weight,
    dense_bias,
    fc1_weight,
    fc1_bias,
    fc2_weight,
    fc2_bias,
    cotangent,
):
    me = lax.axis_index("fsdp")
    core = me % 2
    tp_index = lax.axis_index("tp")
    ctx_index = lax.axis_index("ctx")
    ctx_size = lax.axis_size("ctx")
    shard = ln_gain.shape[0]
    row_count = tokens.shape[1]
    block_rows = row_count // 2
    score_scale = 1.0 / math.sqrt(HD)

    qkv_halves = [
        half_of(qkv_weight, which, 2).reshape(shard, 3 * HD) for which in (core, 1 - core)
    ]
    qkv_full = gather_weight(*qkv_halves)
    dense_full = gather_weight(*[half_of(dense_weight, w, 1) for w in (core, 1 - core)])
    fc1_full = gather_weight(*[half_of(fc1_weight, w, 1) for w in (core, 1 - core)])
    fc2_full = gather_weight(*[half_of(fc2_weight, w, 1) for w in (core, 1 - core)])

    vectors = jnp.stack([ln_gain, ln_bias, dense_bias, fc2_bias])
    vectors = jnp.concatenate([vectors] + [swap(vectors, k) for k in (1, 2, 3)], axis=1)
    norm_gain = vectors[0:1].astype(F32)
    norm_bias = vectors[1:2].astype(F32)
    out_bias = vectors[2:3].astype(F32) + vectors[3:4].astype(F32)

    layout = jnp.concatenate([lengths[0], block_order[0]])
    seq_count = lengths.shape[1]
    layouts = [layout, swap(layout, 1)]
    local_slots = ctx_index * 2 + jnp.arange(2, dtype=jnp.int32)
    if ctx_size == 2:
        key_slots = jnp.concatenate([local_slots, (1 - ctx_index) * 2 + jnp.arange(2)])
    else:
        key_slots = jnp.arange(block_order.shape[1], dtype=jnp.int32)
    allowed, valid, positions = [], [], []
    for each in layouts:
        lengths_row, order_row = each[:seq_count], each[seq_count:]
        local_packed = packed_rows(order_row, local_slots, block_rows)
        key_packed = packed_rows(order_row, key_slots, block_rows)
        segment, position = place_rows(local_packed, lengths_row)
        key_segment = place_rows(key_packed, lengths_row)[0]
        allowed.append(
            (segment[:, None] == key_segment[None, :])
            & (key_packed[None, :] <= local_packed[:, None])
        )
        valid.append((segment < seq_count).astype(F32)[:, None])
        positions.append(position)
    cosine_table, sine_table = rotation_tables(jnp.concatenate(positions))
    valid = jnp.concatenate(valid)

    inputs_low = framed(tokens[0], me)
    upstream_low = framed(cotangent[0], me)

    def normalise(rows):
        rows = rows.astype(F32)
        centred = rows - jnp.mean(rows, axis=1, keepdims=True)
        variance = jnp.mean(centred * centred, axis=1, keepdims=True)
        inverse = lax.rsqrt(variance + NORM_EPSILON)
        return centred * inverse, inverse

    normed_own = (normalise(inputs_low)[0] * norm_gain + norm_bias).astype(BF16)
    swapped = (1, 0, 3, 2)
    normed = jnp.concatenate([normed_own, blocks(swap(normed_own, 1), swapped)])
    upstream = jnp.concatenate([upstream_low, blocks(swap(upstream_low, 1), swapped)])

    projected = dot(normed, qkv_full, ((1,), (0,)))
    qkv_bias_own = half_of(qkv_bias, core, 1).astype(F32).reshape(1, 3 * HD)
    projected = projected + qkv_bias_own
    queries = rotate(projected[:, :HD], cosine_table, sine_table).astype(BF16)
    keys_local = rotate(projected[:, HD : 2 * HD], cosine_table, sine_table).astype(BF16)
    values_local = projected[:, 2 * HD :].astype(BF16)
    both_local = jnp.concatenate([keys_local, values_local], axis=1)
    both_local = both_local.reshape(2, row_count, 2 * HD)
    if ctx_size == 2:
        both_all = jnp.concatenate([both_local, ctx_pair(both_local)], axis=1)
    else:
        both_all = lax.all_gather(both_local, "ctx", axis=1, tiled=True)

    attended, probs_all = [], []
    for s in range(2):
        rows = slice(s * row_count, (s + 1) * row_count)
        keys, values = both_all[s, :, :HD], both_all[s, :, HD:]
        scores = dot(queries[rows], keys, ((1,), (1,))) * score_scale
        scores = jnp.where(allowed[s], scores, MASK_FLOOR)
        exp_scores = jnp.exp(scores - jnp.max(scores, axis=1, keepdims=True))
        probs = exp_scores / jnp.sum(exp_scores, axis=1, keepdims=True)
        probs_all.append(probs)
        attended.append(dot(probs.astype(BF16), values, ((1,), (0,))))
    attended = (jnp.concatenate(attended) * valid).astype(BF16)

    pre_act = dot(normed, fc1_full, ((1,), (0,))) + half_of(fc1_bias, core, 0).astype(F32)[None, :]
    normal_cdf = 0.5 * (1.0 + lax.erf(pre_act * (1.0 / math.sqrt(2.0))))
    density = jnp.exp(-0.5 * pre_act * pre_act) * (1.0 / math.sqrt(2.0 * math.pi))
    hidden = (pre_act * normal_cdf).astype(BF16)
    slope = normal_cdf + pre_act * density

    def share(rows, first, first_weight, second, second_weight, contract):
        return dot(first[rows], first_weight, contract) + dot(second[rows], second_weight, contract)

    own_rows, other_rows = slice(0, row_count), slice(row_count, 2 * row_count)

    def summed(first, first_weight, second, second_weight, contract):
        theirs = share(other_rows, first, first_weight, second, second_weight, contract)
        theirs = swap(blocks(theirs.astype(BF16), swapped), 1)
        own = share(own_rows, first, first_weight, second, second_weight, contract)
        return scatter_rows(own + theirs.astype(F32), tp_index)

    inputs_part = lax.dynamic_slice_in_dim(
        inputs_low, tp_index * (row_count // lax.axis_size("tp")), row_count // lax.axis_size("tp")
    )
    upstream_part = lax.dynamic_slice_in_dim(
        upstream_low,
        tp_index * (row_count // lax.axis_size("tp")),
        row_count // lax.axis_size("tp"),
    ).astype(F32)
    out_part = summed(attended, dense_full, hidden, fc2_full, ((1,), (1,)))
    out_part = (inputs_part.astype(F32) + out_part + out_bias).astype(BF16)
    output = gather_rows(framed(out_part, me), tp_index, BF16)

    fc2_grad = reduce_weight(upstream, hidden)
    hidden_grad = dot(upstream, fc2_full, ((1,), (0,)))
    pre_grad_wide = hidden_grad * slope
    pre_grad = pre_grad_wide.astype(BF16)
    fc1_grad = reduce_weight(normed, pre_grad)
    dense_grad = reduce_weight(upstream, attended)
    attended_grad = (dot(upstream, dense_full, ((1,), (0,))).astype(BF16) * valid.astype(BF16))

    query_pieces, both_pieces = [], []
    for s in range(2):
        rows = slice(s * row_count, (s + 1) * row_count)
        keys, values = both_all[s, :, :HD], both_all[s, :, HD:]
        probs = probs_all[s]
        head_grad = attended_grad[rows]
        prob_grad = dot(head_grad, values, ((1,), (1,)))
        row_delta = jnp.sum(probs * prob_grad, axis=1, keepdims=True)
        score_grad = (probs * (prob_grad - row_delta)).astype(BF16)
        query_pieces.append(dot(score_grad, keys, ((1,), (0,))) * score_scale)
        key_piece = dot(score_grad, queries[rows], ((0,), (0,))) * score_scale
        value_piece = dot(probs.astype(BF16), head_grad, ((0,), (0,)))
        both_pieces.append(jnp.concatenate([key_piece, value_piece], axis=1))
    both_grad = jnp.stack(both_pieces)
    if ctx_size == 2:
        theirs = ctx_pair(both_grad[:, row_count:].astype(BF16))
        both_grad = both_grad[:, :row_count] + theirs.astype(F32)
    else:
        both_grad = lax.psum_scatter(both_grad, "ctx", scatter_dimension=1, tiled=True)
    both_grad = both_grad.reshape(2 * row_count, 2 * HD)
    proj_grad = jnp.concatenate(
        [
            rotate_back(jnp.concatenate(query_pieces), cosine_table, sine_table),
            rotate_back(both_grad[:, :HD], cosine_table, sine_table),
            both_grad[:, HD:],
        ],
        axis=1,
    ).astype(BF16)
    qkv_grad = reduce_weight(normed, proj_grad)

    full_grad = summed(pre_grad, fc1_full, proj_grad, qkv_full, ((1,), (1,)))
    standard, inverse = normalise(inputs_part)
    scaled = full_grad * norm_gain
    input_part = upstream_part + inverse * (
        scaled
        - jnp.mean(scaled, axis=1, keepdims=True)
        - standard * jnp.mean(scaled * standard, axis=1, keepdims=True)
    )
    input_grad = gather_rows(framed(input_part.astype(BF16), me), tp_index, F32)

    column_sums = jnp.concatenate(
        [
            jnp.sum(pre_grad.astype(F32), axis=0, keepdims=True),
            jnp.sum(proj_grad.astype(F32), axis=0, keepdims=True),
        ],
        axis=1,
    )
    column_sums = column_sums + swap(column_sums, 2)
    column_sums = ctx_sum(column_sums)
    column_other = swap(column_sums, 1)
    hidden_half = fc1_bias.shape[0] // 2
    fc1_bias_grad = in_order(column_sums[0, :hidden_half], column_other[0, :hidden_half], core, 0)
    qkv_bias_grad = in_order(
        column_sums[0, hidden_half:].reshape(3, HD), column_other[0, hidden_half:].reshape(3, HD), core, 1
    )

    def to_shard(sums):
        sums = sums[:, : 2 * shard] + swap(sums[:, 2 * shard :], 2)
        sums = sums[:, :shard] + swap(sums[:, shard:], 1)
        return ctx_sum(sums)

    out_bias_grad = to_shard(jnp.sum(upstream_low.astype(F32), axis=0, keepdims=True))[0]
    norm_sums = jnp.concatenate(
        [
            jnp.sum(full_grad * standard, axis=0, keepdims=True),
            jnp.sum(full_grad, axis=0, keepdims=True),
        ]
    )
    norm_sums = to_shard(norm_sums)
    for d in (1, 2):
        norm_sums = norm_sums + lax.ppermute(norm_sums, "tp", [(i, i ^ d) for i in range(4)])

    def whole_columns(halves):
        return in_order(halves[0], halves[1], core, 1)

    qkv_whole = in_order(
        qkv_grad[0].reshape(shard, 3, HD), qkv_grad[1].reshape(shard, 3, HD), core, 2
    )
    return (
        output[None],
        input_grad[None],
        norm_sums[0],
        norm_sums[1],
        qkv_whole,
        qkv_bias_grad,
        whole_columns(dense_grad),
        out_bias_grad,
        whole_columns(fc1_grad),
        fc1_bias_grad,
        whole_columns(fc2_grad),
        out_bias_grad,
    )


def solution(mesh):
    placed = (
        P("fsdp", "ctx", None),
        P("fsdp", None),
        P("fsdp", None),
        P("fsdp"),
        P("fsdp"),
        P("fsdp", None, "tp"),
        P(None, "tp"),
        P("fsdp", "tp"),
        P("fsdp"),
        P("fsdp", "tp"),
        P("tp"),
        P("fsdp", "tp"),
        P("fsdp"),
        P("fsdp", "ctx", None),
    )
    return jax.shard_map(
        per_device,
        mesh=mesh,
        in_specs=placed,
        out_specs=(
            P("fsdp", "ctx", None),
            P("fsdp", "ctx", None),
            P("fsdp"),
            P("fsdp"),
            P("fsdp", None, "tp"),
            P(None, "tp"),
            P("fsdp", "tp"),
            P("fsdp"),
            P("fsdp", "tp"),
            P("tp"),
            P("fsdp", "tp"),
            P("fsdp"),
        ),
        check_vma=False,
    )
```

time: 1220 us -> 615 us (0.50)
  the two profiles are of different devices: /device:TPU:0 before, /device:TPU:9 now
where the time goes in v1:
time: 615 us; the launch traced here: 609 us
  waiting for transfers between devices  303 us (49%)
  other arithmetic  100 us (16%)
  matrix products  86.9 us (14%)
  starting transfers between devices  59.6 us (10%)
  local copies, waits for them, and re-layouts  56.5 us (9%)
    ppermute x34, waiting for transfers between devices, swap(): return lax.ppermute(x, 'fsdp', [(i, i ^ bit) for i in range(size)])  144 us
    dot_general x32, matrix products, dot(): lax.dot_general(a, b, (contract, ((), ())), preferred_element_type=F32)  86.9 us
    ppermute x12, waiting for transfers between devices, tp_shift(): return lax.ppermute(x, 'tp', [(i, (i + d) % size) for i in range(size)])  69.3 us
    ppermute x13, waiting for transfers between devices, ctx_pair(): return lax.ppermute(x, 'ctx', [(0, 1), (1, 0)])  55.5 us
    ppermute x2, waiting for transfers between devices, per_device(): lax.ppermute(norm_sums, 'tp', [(i, i ^ d) for i in range(4)])  34.6 us
    ppermute x34, starting transfers between devices, swap(): return lax.ppermute(x, 'fsdp', [(i, i ^ bit) for i in range(size)])  29 us
    concatenate x1, other arithmetic, per_device(): jnp.concatenate([upstream_low, blocks(swap(upstream_low, 1), swapped)])  28.2 us
    unnamed x178, local copies, waits for them, and re-layouts  22.8 us
  transfers between devices with their start and end apart: 61, of which 22 were waited for; matrix products, arithmetic and copies ran while one was open for 38% of the time, Pallas kernels for 0%

profile of v1, /device:TPU:9, one launch (start us, length us, event | category | flops | bytes accessed | tf_op | source)
XLA Modules:
  0.0 608.6 jit_solution(11339769458575394576)
XLA Ops:
  3.4 1.9 collective-permute-start.2
  6.7 3.8 dynamic-slice_bitcast_fusion.3
  13.1 1.9 convert_reduce_fusion
  17.2 2.6 constant_dynamic-slice_fusion.16
  19.8 2.3 copy.84
  22.1 2.4 copy.83
  26.8 3.2 constant_dynamic-slice_fusion.11
  46.0 28.2 %maximum_maximum_fusion.1 = bf16[1024,2048]{1,0:T(8,128)(2,1)S(1)} fusion(bf16[512,512]{1,0:T(8,128)(2,1)S(1)} %get-tuple-element.86, bf16[512,512]{1,0:T(8,128)(2,1)S(1)} %get-tuple-element.87, bf16[512,512]{1,0:T(8,128)(2,1)S(1)} %get-tuple-element.88, bf16[512,512]{1,0:T(8,128)(2,1)S(1)} %get-tuple-element.85, bf16[512,512]{1,0:T(8,128)(2,1)S(1)} %copy-done.9, ...), kind=kLoop, calls=%fused_computation.18 | loop fusion | flops 33554432 | bytes 8388608 | tf_op jit(solution)/shard_map/concatenate | solution.py:218
  76.5 2.0 fusion.57
  78.8 15.7 %maximum_maximum_fusion = bf16[1024,2048]{1,0:T(8,128)(2,1)S(1)} fusion(bf16[512,512]{1,0:T(8,128)(2,1)S(1)} %get-tuple-element.102, bf16[512,512]{1,0:T(8,128)(2,1)S(1)} %get-tuple-element.103, bf16[512,512]{1,0:T(8,128)(2,1)S(1)} %get-tuple-element.104, bf16[512,512]{1,0:T(8,128)(2,1)S(1)} %get-tuple-element.101, bf16[512,2048]{1,0:T(8,128)(2,1)S(1)} %fusion.5), kind=kLoop, calls=%fused_computation.15 | loop fusion | flops 20971520 | bytes 8388608 | tf_op jit(solution)/shard_map/concatenate | solution.py:217
  96.6 3.4 fusion.177
  101.9 15.6 %collective-permute-done.14 = bf16[512,1024]{1,0:T(8,128)(2,1)} collective-permute-done((bf16[512,1024]{1,0:T(8,128)(2,1)}, bf16[512,1024]{1,0:T(8,128)(2,1)}, u32[]{:S(2)}, u32[]{:S(2)}) %collective-permute-start.14) | collective-permute-done | bytes 1048608 | tf_op jit(solution)/shard_map/ppermute | solution.py:62
  118.3 42.3 %collective-permute-done.13 = bf16[512,1024]{1,0:T(8,128)(2,1)} collective-permute-done((bf16[512,1024]{1,0:T(8,128)(2,1)S(1)}, bf16[512,1024]{1,0:T(8,128)(2,1)}, u32[]{:S(2)}, u32[]{:S(2)}) %collective-permute-start.13) | collective-permute-done | bytes 1048608 | tf_op jit(solution)/shard_map/ppermute | solution.py:62
  161.8 9.7 %multiply_convert_fusion = (bf16[1024,1024]{1,0:T(8,128)(2,1)S(1)}, f32[1024,1024]{1,0:T(8,128)S(1)}) fusion(f32[1024]{0:T(1024)} %dynamic-slice_convert_fusion.6, bf16[1024,2048]{1,0:T(8,128)(2,1)} %copy-done.12, bf16[512,1024]{1,0:T(8,128)(2,1)} %collective-permute-done.14, bf16[512,1024]{1,0:T(8,128)(2,1)} %collective-permute-done.13, ...), kind=kOutput, calls=%fused_computation.31 | convolution fusion | flops 4318035968 | bytes 14684160 | tf_op jit(solution)/shard_map/dot_general | solution.py:57
  171.5 11.4 %collective-permute-done.16 = bf16[512,1024]{1,0:T(8,128)(2,1)S(1)} collective-permute-done((bf16[512,1024]{1,0:T(8,128)(2,1)}, bf16[512,1024]{1,0:T(8,128)(2,1)S(1)}, u32[]{:S(2)}, u32[]{:S(2)}) %collective-permute-start.16) | collective-permute-done | bytes 1048608 | tf_op jit(solution)/shard_map/ppermute | solution.py:62
  183.0 7.4 %convert_reduce_fusion.2 = (f32[1024]{0:T(1024)S(1)}, bf16[1024,1024]{1,0:T(8,128)(2,1)S(1)}) fusion(f32[1024,1024]{1,0:T(8,128)S(1)} %get-tuple-element.142, f32[1024]{0:T(1024)S(1)} %copy-done.65, bf16[1024,2048]{1,0:T(8,128)(2,1)S(1)} %copy-done.16, bf16[512,1024]{1,0:T(8,128)(2,1)} %collective-permute-done.17, ...), kind=kOutput, calls=%fused_computation.26 | convolution fusion | flops 4325374976 | bytes 14688256 | tf_op jit(solution)/shard_map/dot_general | solution.py:57
  190.5 3.8 convolution_convert_fusion.1
  195.0 3.8 convolution_convert_fusion
  199.5 5.8 fusion.69
  206.4 5.9 fusion.71
  229.4 67.0 %collective-permute-done.46 = bf16[1024,256]{0,1:T(8,128)(2,1)S(1)} collective-permute-done((bf16[1024,256]{0,1:T(8,128)(2,1)S(1)}, bf16[1024,256]{0,1:T(8,128)(2,1)S(1)}, u32[]{:S(2)}, u32[]{:S(2)}) %collective-permute-start.46) | collective-permute-done | bytes 524320 | tf_op jit(solution)/shard_map/ppermute | solution.py:62
  297.3 2.3 collective-permute-start.48
  302.8 4.6 collective-permute-done.47
  310.6 3.0 fusion.34
  317.0 5.3 add_convert_fusion.1
  328.2 4.2 add_convert_fusion.2
  332.6 4.2 fusion.77
  339.8 4.0 add_convert_fusion
  343.8 5.3 collective-permute-done.43
  351.1 11.3 %collective-permute-done.44 = f32[1,1792]{1,0:T(1,128)S(1)} collective-permute-done((f32[1,1792]{1,0:T(1,128)S(1)}, f32[1,1792]{1,0:T(1,128)S(1)}, u32[]{:S(2)}, u32[]{:S(2)}) %collective-permute-start.44) | collective-permute-done | bytes 7200 | tf_op jit(solution)/shard_map/ppermute | solution.py:66
  362.3 2.3 collective-permute-start.45
  368.2 3.0 convert_add_fusion.1
  376.1 15.7 %collective-permute-done.58 = bf16[512,1024]{0,1:T(8,128)(2,1)S(1)} collective-permute-done((bf16[512,1024]{0,1:T(8,128)(2,1)}, bf16[512,1024]{0,1:T(8,128)(2,1)S(1)}, u32[]{:S(2)}, u32[]{:S(2)}) %collective-permute-start.58) | collective-permute-done | bytes 1048608 | tf_op jit(solution)/shard_map/ppermute | solution.py:66
  392.2 3.4 add_convert_fusion.4
  398.0 2.0 collective-permute-start.41
  401.1 5.6 convert_add_fusion
  408.2 6.1 %collective-permute-done.56 = bf16[512,1024]{0,1:T(8,128)(2,1)S(1)} collective-permute-done((bf16[512,1024]{0,1:T(8,128)(2,1)}, bf16[512,1024]{0,1:T(8,128)(2,1)S(1)}, u32[]{:S(2)}, u32[]{:S(2)}) %collective-permute-start.56) | collective-permute-done | bytes 1048608 | tf_op jit(solution)/shard_map/ppermute | solution.py:66
  414.4 2.3 collective-permute-start.29
  418.2 2.9 maximum_select_fusion
  421.1 15.7 %collective-permute-done.60 = bf16[512,1024]{0,1:T(8,128)(2,1)S(1)} collective-permute-done((bf16[512,1024]{0,1:T(8,128)(2,1)}, bf16[512,1024]{0,1:T(8,128)(2,1)S(1)}, u32[]{:S(2)}, u32[]{:S(2)}) %collective-permute-start.60) | collective-permute-done | bytes 1048608 | tf_op jit(solution)/shard_map/ppermute | solution.py:66
  438.0 2.9 convert_add_fusion.2
  440.9 5.6 copy.74
  446.5 5.3 maximum_select_fusion.1
  451.7 5.5 copy.75
  457.4 2.6 convert_add_fusion.7
  460.0 3.2 copy.66
  463.1 2.4 collective-permute-start.20
  467.5 2.4 fusion.63
  469.9 23.8 %collective-permute-done.20 = bf16[128,2048]{1,0:T(8,128)(2,1)S(1)} collective-permute-done((bf16[128,2048]{1,0:T(8,128)(2,1)}, bf16[128,2048]{1,0:T(8,128)(2,1)S(1)}, u32[]{:S(2)}, u32[]{:S(2)}) %collective-permute-start.20) | collective-permute-done | bytes 524320 | tf_op jit(solution)/shard_map/ppermute | solution.py:77
  493.7 11.1 %collective-permute-done.19 = bf16[128,2048]{1,0:T(8,128)(2,1)S(1)} collective-permute-done((bf16[128,2048]{1,0:T(8,128)(2,1)S(1)}, bf16[128,2048]{1,0:T(8,128)(2,1)S(1)}, u32[]{:S(2)}, u32[]{:S(2)}) %collective-permute-start.19) | collective-permute-done | bytes 524320 | tf_op jit(solution)/shard_map/ppermute | solution.py:77
  504.8 2.4 fusion.62
  509.0 2.2 collective-permute-start.22
  517.4 2.6 collective-permute-start.37
  520.9 23.3 %collective-permute-done.37 = f32[2,512]{1,0:T(2,128)S(1)} collective-permute-done((f32[2,512]{1,0:T(2,128)S(1)}, f32[2,512]{1,0:T(2,128)S(1)}, u32[]{:S(2)}, u32[]{:S(2)}) %collective-permute-start.37) | collective-permute-done | bytes 4128 | tf_op jit(solution)/shard_map/ppermute | solution.py:352
  544.5 11.3 %collective-permute-done.38 = f32[2,512]{1,0:T(2,128)S(1)} collective-permute-done((f32[2,512]{1,0:T(2,128)S(1)}, f32[2,512]{1,0:T(2,128)S(1)}, u32[]{:S(2)}, u32[]{:S(2)}) %collective-permute-start.38) | collective-permute-done | bytes 4128 | tf_op jit(solution)/shard_map/ppermute | solution.py:352
  556.4 3.4 collective-permute-start.32
  562.9 4.6 collective-permute-done.31
  567.5 2.1 convert_dynamic-update-slice_fusion.2
  569.6 1.9 bitcast_dynamic-update-slice_fusion
  571.5 2.3 maximum_select_fusion.2
  573.8 26.5 %collective-permute-done.32 = bf16[128,2048]{1,0:T(8,128)(2,1)} collective-permute-done((bf16[128,2048]{1,0:T(8,128)(2,1)}, bf16[128,2048]{1,0:T(8,128)(2,1)}, u32[]{:S(2)}, u32[]{:S(2)}) %collective-permute-start.32) | collective-permute-done | bytes 524320 | tf_op jit(solution)/shard_map/ppermute | solution.py:77
  600.2 2.1 convert_dynamic-update-slice_fusion.1
  602.4 3.3 collective-permute-done.33
  605.7 2.1 convert_dynamic-update-slice_fusion
  (419 shorter events, 108.1 us)
Async XLA Ops:
  3.4 33.2 %collective-permute-start.2 = (bf16[4,512]{1,0:T(4,128)(2,1)S(1)}, bf16[4,512]{1,0:T(4,128)(2,1)S(1)}, u32[]{:S(2)}, u32[]{:S(2)}) collective-permute-start(bf16[4,512]{1,0:T(4,128)(2,1)S(1)} %pad_maximum_fusion.18), channel_id=1, source_target_pairs={{0,24},{8,16},{16,8},{24,0},{1,25},{9,17},{17,9},{25,1},{2,26},{10... | collective-permute-start | bytes 12296 | tf_op jit(solution)/shard_map/ppermute | solution.py:62
  5.3 31.4 %collective-permute-start.1 = (bf16[4,512]{1,0:T(4,128)(2,1)S(1)}, bf16[4,512]{1,0:T(4,128)(2,1)S(1)}, u32[]{:S(2)}, u32[]{:S(2)}) collective-permute-start(bf16[4,512]{1,0:T(4,128)(2,1)S(1)} %pad_maximum_fusion.18), channel_id=1, source_target_pairs={{0,16},{8,24},{16,0},{24,8},{1,17},{9,25},{17,1},{25,9},{2,18},{10... | collective-permute-start | bytes 12296 | tf_op jit(solution)/shard_map/ppermute | solution.py:62
  5.5 31.7 %collective-permute-start = (bf16[4,512]{1,0:T(4,128)(2,1)S(1)}, bf16[4,512]{1,0:T(4,128)(2,1)S(1)}, u32[]{:S(2)}, u32[]{:S(2)}) collective-permute-start(bf16[4,512]{1,0:T(4,128)(2,1)S(1)} %pad_maximum_fusion.18), channel_id=1, source_target_pairs={{0,8},{8,0},{16,24},{24,16},{1,9},{9,1},{17,25},{25,17},{2,10},{10... | collective-permute-start | bytes 12296 | tf_op jit(solution)/shard_map/ppermute | solution.py:62
  6.5 25.1 %collective-permute-start.7 = (s32[7]{0:T(128)S(1)}, s32[7]{0:T(128)S(1)}, u32[]{:S(2)}, u32[]{:S(2)}) collective-permute-start(s32[7]{0:T(128)S(1)} %pad_add_fusion.1), channel_id=1, source_target_pairs={{0,8},{8,0},{16,24},{24,16},{1,9},{9,1},{17,25},{25,17},{2,10},{10... | collective-permute-start | bytes 92 | tf_op jit(solution)/shard_map/ppermute | solution.py:62
  12.3 31.3 %collective-permute-start.25 = (bf16[512,2048]{1,0:T(8,128)(2,1)}, bf16[512,2048]{1,0:T(8,128)(2,1)}, u32[]{:S(2)}, u32[]{:S(2)}) collective-permute-start(bf16[512,2048]{1,0:T(8,128)(2,1)} %get-tuple-element.61), channel_id=1, source_target_pairs={{0,8},{8,0},{16,24},{24,16},{1,9},{9,1},{17,25},{25,17},{2,10},{10... | collective-permute-start | bytes 6291464 | tf_op jit(solution)/shard_map/ppermute | solution.py:62
  31.6 3.7 collective-permute-start.50
  35.3 39.0 %collective-permute-start.11 = (bf16[512,256]{1,0:T(8,128)(2,1)}, bf16[512,256]{1,0:T(8,128)(2,1)S(1)}, u32[]{:S(2)}, u32[]{:S(2)}) collective-permute-start(bf16[512,256]{1,0:T(8,128)(2,1)} %get-tuple-element.124), channel_id=1, source_target_pairs={{0,24},{8,16},{16,8},{24,0},{1,25},{9,17},{17,9},{25,1},{2,26},{10... | collective-permute-start | bytes 786440 | tf_op jit(solution)/shard_map/ppermute | solution.py:62
  36.6 38.6 %collective-permute-start.9 = (bf16[512,256]{1,0:T(8,128)(2,1)}, bf16[512,256]{1,0:T(8,128)(2,1)S(1)}, u32[]{:S(2)}, u32[]{:S(2)}) collective-permute-start(bf16[512,256]{1,0:T(8,128)(2,1)} %get-tuple-element.124), channel_id=1, source_target_pairs={{0,8},{8,0},{16,24},{24,16},{1,9},{9,1},{17,25},{25,17},{2,10},{10... | collective-permute-start | bytes 786440 | tf_op jit(solution)/shard_map/ppermute | solution.py:62
  36.7 1.7 collective-permute-start.51
  38.2 40.4 %collective-permute-start.3 = (bf16[512,2048]{1,0:T(8,128)(2,1)S(1)}, bf16[512,2048]{1,0:T(8,128)(2,1)S(1)}, u32[]{:S(2)}, u32[]{:S(2)}) collective-permute-start(bf16[512,2048]{1,0:T(8,128)(2,1)S(1)} %fusion.5), channel_id=1, source_target_pairs={{0,8},{8,0},{16,24},{24,16},{1,9},{9,1},{17,25},{25,17},{2,10},{10... | collective-permute-start | bytes 6291464 | tf_op jit(solution)/shard_map/ppermute | solution.py:62
  38.4 2.7 collective-permute-start.52
  41.2 53.4 %collective-permute-start.6 = (bf16[512,768]{0,1:T(8,128)(2,1)S(1)}, bf16[512,768]{0,1:T(8,128)(2,1)S(1)}, u32[]{:S(2)}, u32[]{:S(2)}) collective-permute-start(bf16[512,768]{0,1:T(8,128)(2,1)S(1)} %bitcast.140), channel_id=1, source_target_pairs={{0,24},{8,16},{16,8},{24,0},{1,25},{9,17},{17,9},{25,1},{2,26},{10... | collective-permute-start | bytes 2359304 | tf_op jit(solution)/shard_map/ppermute | solution.py:62
  43.6 30.7 %collective-permute-start.10 = (bf16[512,256]{1,0:T(8,128)(2,1)S(1)}, bf16[512,256]{1,0:T(8,128)(2,1)S(1)}, u32[]{:S(2)}, u32[]{:S(2)}) collective-permute-start(bf16[512,256]{1,0:T(8,128)(2,1)S(1)} %get-tuple-element.123), channel_id=1, source_target_pairs={{0,16},{8,24},{16,0},{24,8},{1,17},{9,25},{17,1},{25,9},{2,18},{10... | collective-permute-start | bytes 786440 | tf_op jit(solution)/shard_map/ppermute | solution.py:62
  74.3 21.5 %collective-permute-start.4 = (bf16[512,768]{0,1:T(8,128)(2,1)S(1)}, bf16[512,768]{0,1:T(8,128)(2,1)S(1)}, u32[]{:S(2)}, u32[]{:S(2)}) collective-permute-start(bf16[512,768]{0,1:T(8,128)(2,1)S(1)} %bitcast.141), channel_id=1, source_target_pairs={{0,8},{8,0},{16,24},{24,16},{1,9},{9,1},{17,25},{25,17},{2,10},{10... | collective-permute-start | bytes 2359304 | tf_op jit(solution)/shard_map/ppermute | solution.py:62
  74.4 21.4 %collective-permute-start.5 = (bf16[512,768]{0,1:T(8,128)(2,1)S(1)}, bf16[512,768]{0,1:T(8,128)(2,1)S(1)}, u32[]{:S(2)}, u32[]{:S(2)}) collective-permute-start(bf16[512,768]{0,1:T(8,128)(2,1)S(1)} %bitcast.136), channel_id=1, source_target_pairs={{0,16},{8,24},{16,0},{24,8},{1,17},{9,25},{17,1},{25,9},{2,18},{10... | collective-permute-start | bytes 2359304 | tf_op jit(solution)/shard_map/ppermute | solution.py:62
  75.2 42.3 %collective-permute-start.14 = (bf16[512,1024]{1,0:T(8,128)(2,1)}, bf16[512,1024]{1,0:T(8,128)(2,1)}, u32[]{:S(2)}, u32[]{:S(2)}) collective-permute-start(bf16[512,1024]{1,0:T(8,128)(2,1)} %get-tuple-element.100), channel_id=1, source_target_pairs={{0,24},{8,16},{16,8},{24,0},{1,25},{9,17},{17,9},{25,1},{2,26},{10... | collective-permute-start | bytes 3145736 | tf_op jit(solution)/shard_map/ppermute | solution.py:62
  78.6 83.2 %collective-permute-start.12 = (bf16[512,1024]{1,0:T(8,128)(2,1)}, bf16[512,1024]{1,0:T(8,128)(2,1)}, u32[]{:S(2)}, u32[]{:S(2)}) collective-permute-start(bf16[512,1024]{1,0:T(8,128)(2,1)} %get-tuple-element.100), channel_id=1, source_target_pairs={{0,8},{8,0},{16,24},{24,16},{1,9},{9,1},{17,25},{25,17},{2,10},{10... | collective-permute-start | bytes 3145736 | tf_op jit(solution)/shard_map/ppermute | solution.py:62
  94.6 76.9 %collective-permute-start.17 = (bf16[512,1024]{1,0:T(8,128)(2,1)}, bf16[512,1024]{1,0:T(8,128)(2,1)}, u32[]{:S(2)}, u32[]{:S(2)}) collective-permute-start(bf16[512,1024]{1,0:T(8,128)(2,1)} %get-tuple-element.98), channel_id=1, source_target_pairs={{0,24},{8,16},{16,8},{24,0},{1,25},{9,17},{17,9},{25,1},{2,26},{10... | collective-permute-start | bytes 3145736 | tf_op jit(solution)/shard_map/ppermute | solution.py:62
  95.8 87.2 %collective-permute-start.15 = (bf16[512,1024]{1,0:T(8,128)(2,1)}, bf16[512,1024]{1,0:T(8,128)(2,1)}, u32[]{:S(2)}, u32[]{:S(2)}) collective-permute-start(bf16[512,1024]{1,0:T(8,128)(2,1)} %get-tuple-element.98), channel_id=1, source_target_pairs={{0,8},{8,0},{16,24},{24,16},{1,9},{9,1},{17,25},{25,17},{2,10},{10... | collective-permute-start | bytes 3145736 | tf_op jit(solution)/shard_map/ppermute | solution.py:62
  95.8 64.8 %collective-permute-start.13 = (bf16[512,1024]{1,0:T(8,128)(2,1)S(1)}, bf16[512,1024]{1,0:T(8,128)(2,1)}, u32[]{:S(2)}, u32[]{:S(2)}) collective-permute-start(bf16[512,1024]{1,0:T(8,128)(2,1)S(1)} %copy-done.30), channel_id=1, source_target_pairs={{0,16},{8,24},{16,0},{24,8},{1,17},{9,25},{17,1},{25,9},{2,18},{10... | collective-permute-start | bytes 3145736 | tf_op jit(solution)/shard_map/ppermute | solution.py:62
  117.5 65.4 %collective-permute-start.16 = (bf16[512,1024]{1,0:T(8,128)(2,1)}, bf16[512,1024]{1,0:T(8,128)(2,1)S(1)}, u32[]{:S(2)}, u32[]{:S(2)}) collective-permute-start(bf16[512,1024]{1,0:T(8,128)(2,1)} %get-tuple-element.97), channel_id=1, source_target_pairs={{0,16},{8,24},{16,0},{24,8},{1,17},{9,25},{17,1},{25,9},{2,18},{10... | collective-permute-start | bytes 3145736 | tf_op jit(solution)/shard_map/ppermute | solution.py:62
  160.6 51.7 %collective-permute-start.8 = (bf16[2,512,512]{2,1,0:T(8,128)(2,1)S(1)}, bf16[2,512,512]{2,1,0:T(8,128)(2,1)S(1)}, u32[]{:S(2)}, u32[]{:S(2)}) collective-permute-start(bf16[2,512,512]{2,1,0:T(8,128)(2,1)S(1)} %bitcast.119), channel_id=1, source_target_pairs={{0,4},{4,0},{1,5},{5,1},{2,6},{6,2},{3,7},{7,3},{8,12},{12,8},{9,1... | collective-permute-start | bytes 3145736 | tf_op jit(solution)/shard_map/ppermute | solution.py:66
  190.4 124.3 %copy-start.52 = (f32[1024]{0:T(1024)}, f32[1024]{0:T(1024)S(1)}, u32[]{:S(2)}) copy-start(f32[1024]{0:T(1024)S(1)} %get-tuple-element.143) | copy-start | bytes 12292
  194.2 122.8 %collective-permute-start.53 = (bf16[1024,1024]{0,1:T(8,128)(2,1)}, bf16[1024,1024]{0,1:T(8,128)(2,1)}, u32[]{:S(2)}, u32[]{:S(2)}) collective-permute-start(bf16[1024,1024]{0,1:T(8,128)(2,1)} %convolution_convert_fusion.1), channel_id=1, source_target_pairs={{0,16},{8,24},{16,0},{24,8},{1,17},{9,25},{17,1},{25,9},{2,18},{10... | collective-permute-start | bytes 6291464 | tf_op jit(solution)/shard_map/ppermute | solution.py:62
  198.8 139.8 %collective-permute-start.57 = (bf16[1024,1024]{0,1:T(8,128)(2,1)}, bf16[1024,1024]{0,1:T(8,128)(2,1)}, u32[]{:S(2)}, u32[]{:S(2)}) collective-permute-start(bf16[1024,1024]{0,1:T(8,128)(2,1)} %convolution_convert_fusion), channel_id=1, source_target_pairs={{0,16},{8,24},{16,0},{24,8},{1,17},{9,25},{17,1},{25,9},{2,18},{10... | collective-permute-start | bytes 6291464 | tf_op jit(solution)/shard_map/ppermute | solution.py:62
  222.5 86.1 %collective-permute-start.26 = (bf16[2,512,512]{1,2,0:T(8,128)(2,1)S(1)}, bf16[2,512,512]{1,2,0:T(8,128)(2,1)S(1)}, u32[]{:S(2)}, u32[]{:S(2)}) collective-permute-start(bf16[2,512,512]{1,2,0:T(8,128)(2,1)S(1)} %fusion.15), channel_id=1, source_target_pairs={{0,4},{4,0},{1,5},{5,1},{2,6},{6,2},{3,7},{7,3},{8,12},{12,8},{9,1... | collective-permute-start | bytes 3145736 | tf_op jit(solution)/shard_map/ppermute | solution.py:66
  224.6 71.9 %copy-start.21 = (bf16[1024,256]{1,0:T(8,128)(2,1)}, bf16[1024,256]{1,0:T(8,128)(2,1)S(1)}, u32[]{:S(2)}) copy-start(bf16[1024,256]{1,0:T(8,128)(2,1)S(1)} %fusion.73) | copy-start | bytes 1572868
  225.3 71.1 %collective-permute-start.46 = (bf16[1024,256]{0,1:T(8,128)(2,1)S(1)}, bf16[1024,256]{0,1:T(8,128)(2,1)S(1)}, u32[]{:S(2)}, u32[]{:S(2)}) collective-permute-start(bf16[1024,256]{0,1:T(8,128)(2,1)S(1)} %fusion.46), channel_id=1, source_target_pairs={{0,16},{8,24},{16,0},{24,8},{1,17},{9,25},{17,1},{25,9},{2,18},{10... | collective-permute-start | bytes 1572872 | tf_op jit(solution)/shard_map/ppermute | solution.py:62
  297.3 5.1 collective-permute-start.48
  299.6 7.8 %collective-permute-start.47 = (bf16[512,256]{0,1:T(8,128)(2,1)S(1)}, bf16[512,256]{0,1:T(8,128)(2,1)S(1)}, u32[]{:S(2)}, u32[]{:S(2)}) collective-permute-start(bf16[512,256]{0,1:T(8,128)(2,1)S(1)} %get-tuple-element.113), channel_id=1, source_target_pairs={{0,4},{4,0},{1,5},{5,1},{2,6},{6,2},{3,7},{7,3},{8,12},{12,8},{9,1... | collective-permute-start | bytes 786440 | tf_op jit(solution)/shard_map/ppermute | solution.py:66
  302.4 64.6 %collective-permute-start.18 = (bf16[512,2048]{1,0:T(8,128)(2,1)}, bf16[512,2048]{1,0:T(8,128)(2,1)S(1)}, u32[]{:S(2)}, u32[]{:S(2)}) collective-permute-start(bf16[512,2048]{1,0:T(8,128)(2,1)} %pad_maximum_fusion.5), channel_id=1, source_target_pairs={{0,8},{8,0},{16,24},{24,16},{1,9},{9,1},{17,25},{25,17},{2,10},{10... | collective-permute-start | bytes 6291464 | tf_op jit(solution)/shard_map/ppermute | solution.py:62
  307.3 7.4 %collective-permute-start.49 = (bf16[512,256]{0,1:T(8,128)(2,1)S(1)}, bf16[512,256]{0,1:T(8,128)(2,1)S(1)}, u32[]{:S(2)}, u32[]{:S(2)}) collective-permute-start(bf16[512,256]{0,1:T(8,128)(2,1)S(1)} %collective-permute-done.48), channel_id=1, source_target_pairs={{0,4},{4,0},{1,5},{5,1},{2,6},{6,2},{3,7},{7,3},{8,12},{12,8},{9,1... | collective-permute-start | bytes 786440 | tf_op jit(solution)/shard_map/ppermute | solution.py:66
  313.9 78.2 %collective-permute-start.39 = (bf16[1024,768]{0,1:T(8,128)(2,1)}, bf16[1024,768]{0,1:T(8,128)(2,1)}, u32[]{:S(2)}, u32[]{:S(2)}) collective-permute-start(bf16[1024,768]{0,1:T(8,128)(2,1)} %fusion.34), channel_id=1, source_target_pairs={{0,16},{8,24},{16,0},{24,8},{1,17},{9,25},{17,1},{25,9},{2,18},{10... | collective-permute-start | bytes 4718600 | tf_op jit(solution)/shard_map/ppermute | solution.py:62
  314.8 34.4 %collective-permute-start.43 = (f32[1,1792]{1,0:T(1,128)S(1)}, f32[1,1792]{1,0:T(1,128)S(1)}, u32[]{:S(2)}, u32[]{:S(2)}) collective-permute-start(f32[1,1792]{1,0:T(1,128)S(1)} %pad_maximum_fusion.17), channel_id=1, source_target_pairs={{0,16},{8,24},{16,0},{24,8},{1,17},{9,25},{17,1},{25,9},{2,18},{10... | collective-permute-start | bytes 21512 | tf_op jit(solution)/shard_map/ppermute | solution.py:62
  324.5 42.7 %collective-permute-start.55 = (bf16[512,1024]{0,1:T(8,128)(2,1)}, bf16[512,1024]{0,1:T(8,128)(2,1)}, u32[]{:S(2)}, u32[]{:S(2)}) collective-permute-start(bf16[512,1024]{0,1:T(8,128)(2,1)} %get-tuple-element.78), channel_id=1, source_target_pairs={{0,8},{8,0},{16,24},{24,16},{1,9},{9,1},{17,25},{25,17},{2,10},{10... | collective-permute-start | bytes 3145736 | tf_op jit(solution)/shard_map/ppermute | solution.py:62
  338.6 33.9 %collective-permute-start.54 = (bf16[512,1024]{0,1:T(8,128)(2,1)}, bf16[512,1024]{0,1:T(8,128)(2,1)}, u32[]{:S(2)}, u32[]{:S(2)}) collective-permute-start(bf16[512,1024]{0,1:T(8,128)(2,1)} %get-tuple-element.77), channel_id=1, source_target_pairs={{0,4},{4,0},{1,5},{5,1},{2,6},{6,2},{3,7},{7,3},{8,12},{12,8},{9,1... | collective-permute-start | bytes 3145736 | tf_op jit(solution)/shard_map/ppermute | solution.py:66
  349.2 13.1 %collective-permute-start.44 = (f32[1,1792]{1,0:T(1,128)S(1)}, f32[1,1792]{1,0:T(1,128)S(1)}, u32[]{:S(2)}, u32[]{:S(2)}) collective-permute-start(f32[1,1792]{1,0:T(1,128)S(1)} %fusion.155), channel_id=1, source_target_pairs={{0,4},{4,0},{1,5},{5,1},{2,6},{6,2},{3,7},{7,3},{8,12},{12,8},{9,1... | collective-permute-start | bytes 21512 | tf_op jit(solution)/shard_map/ppermute | solution.py:66
  362.3 3.1 collective-permute-start.45
  365.4 7.5 %collective-permute-start.59 = (bf16[512,1024]{0,1:T(8,128)(2,1)}, bf16[512,1024]{0,1:T(8,128)(2,1)}, u32[]{:S(2)}, u32[]{:S(2)}) collective-permute-start(bf16[512,1024]{0,1:T(8,128)(2,1)} %get-tuple-element.76), channel_id=1, source_target_pairs={{0,8},{8,0},{16,24},{24,16},{1,9},{9,1},{17,25},{25,17},{2,10},{10... | collective-permute-start | bytes 3145736 | tf_op jit(solution)/shard_map/ppermute | solution.py:62
  367.0 34.0 %collective-permute-start.27 = (bf16[512,2048]{1,0:T(8,128)(2,1)}, bf16[512,2048]{1,0:T(8,128)(2,1)S(1)}, u32[]{:S(2)}, u32[]{:S(2)}) collective-permute-start(bf16[512,2048]{1,0:T(8,128)(2,1)} %pad_maximum_fusion.7), channel_id=1, source_target_pairs={{0,8},{8,0},{16,24},{24,16},{1,9},{9,1},{17,25},{25,17},{2,10},{10... | collective-permute-start | bytes 6291464 | tf_op jit(solution)/shard_map/ppermute | solution.py:62
  367.2 24.6 %collective-permute-start.58 = (bf16[512,1024]{0,1:T(8,128)(2,1)}, bf16[512,1024]{0,1:T(8,128)(2,1)S(1)}, u32[]{:S(2)}, u32[]{:S(2)}) collective-permute-start(bf16[512,1024]{0,1:T(8,128)(2,1)} %get-tuple-element.75), channel_id=1, source_target_pairs={{0,4},{4,0},{1,5},{5,1},{2,6},{6,2},{3,7},{7,3},{8,12},{12,8},{9,1... | collective-permute-start | bytes 3145736 | tf_op jit(solution)/shard_map/ppermute | solution.py:66
  372.5 41.9 %collective-permute-start.56 = (bf16[512,1024]{0,1:T(8,128)(2,1)}, bf16[512,1024]{0,1:T(8,128)(2,1)S(1)}, u32[]{:S(2)}, u32[]{:S(2)}) collective-permute-start(bf16[512,1024]{0,1:T(8,128)(2,1)} %collective-permute-done.55), channel_id=1, source_target_pairs={{0,4},{4,0},{1,5},{5,1},{2,6},{6,2},{3,7},{7,3},{8,12},{12,8},{9,1... | collective-permute-start | bytes 3145736 | tf_op jit(solution)/shard_map/ppermute | solution.py:66
  372.9 63.8 %collective-permute-start.60 = (bf16[512,1024]{0,1:T(8,128)(2,1)}, bf16[512,1024]{0,1:T(8,128)(2,1)S(1)}, u32[]{:S(2)}, u32[]{:S(2)}) collective-permute-start(bf16[512,1024]{0,1:T(8,128)(2,1)} %collective-permute-done.59), channel_id=1, source_target_pairs={{0,4},{4,0},{1,5},{5,1},{2,6},{6,2},{3,7},{7,3},{8,12},{12,8},{9,1... | collective-permute-start | bytes 3145736 | tf_op jit(solution)/shard_map/ppermute | solution.py:66
  398.0 65.1 %collective-permute-start.41 = (bf16[512,768]{0,1:T(8,128)(2,1)}, bf16[512,768]{0,1:T(8,128)(2,1)S(1)}, u32[]{:S(2)}, u32[]{:S(2)}) collective-permute-start(bf16[512,768]{0,1:T(8,128)(2,1)} %get-tuple-element.110), channel_id=1, source_target_pairs={{0,8},{8,0},{16,24},{24,16},{1,9},{9,1},{17,25},{25,17},{2,10},{10... | collective-permute-start | bytes 2359304 | tf_op jit(solution)/shard_map/ppermute | solution.py:62
  400.0 57.1 %collective-permute-start.40 = (bf16[512,768]{0,1:T(8,128)(2,1)}, bf16[512,768]{0,1:T(8,128)(2,1)}, u32[]{:S(2)}, u32[]{:S(2)}) collective-permute-start(bf16[512,768]{0,1:T(8,128)(2,1)} %get-tuple-element.109), channel_id=1, source_target_pairs={{0,4},{4,0},{1,5},{5,1},{2,6},{6,2},{3,7},{7,3},{8,12},{12,8},{9,1... | collective-permute-start | bytes 2359304 | tf_op jit(solution)/shard_map/ppermute | solution.py:66
  408.1 57.5 %collective-permute-start.30 = (bf16[128,2048]{1,0:T(8,128)(2,1)}, bf16[128,2048]{1,0:T(8,128)(2,1)}, u32[]{:S(2)}, u32[]{:S(2)}) collective-permute-start(bf16[128,2048]{1,0:T(8,128)(2,1)} %get-tuple-element.66), channel_id=1, source_target_pairs={{0,3},{1,0},{2,1},{3,2},{4,7},{5,4},{6,5},{7,6},{8,11},{9,8},{10,9... | collective-permute-start | bytes 1572872 | tf_op jit(solution)/shard_map/ppermute | solution.py:77
  414.4 52.1 %collective-permute-start.29 = (bf16[128,2048]{1,0:T(8,128)(2,1)}, bf16[128,2048]{1,0:T(8,128)(2,1)}, u32[]{:S(2)}, u32[]{:S(2)}) collective-permute-start(bf16[128,2048]{1,0:T(8,128)(2,1)} %get-tuple-element.67), channel_id=1, source_target_pairs={{0,2},{1,3},{2,0},{3,1},{4,6},{5,7},{6,4},{7,5},{8,10},{9,11},{10,... | collective-permute-start | bytes 1572872 | tf_op jit(solution)/shard_map/ppermute | solution.py:77
  436.7 30.7 %collective-permute-start.28 = (bf16[128,2048]{1,0:T(8,128)(2,1)}, bf16[128,2048]{1,0:T(8,128)(2,1)}, u32[]{:S(2)}, u32[]{:S(2)}) collective-permute-start(bf16[128,2048]{1,0:T(8,128)(2,1)} %get-tuple-element.65), channel_id=1, source_target_pairs={{0,1},{1,2},{2,3},{3,0},{4,5},{5,6},{6,7},{7,4},{8,9},{9,10},{10,1... | collective-permute-start | bytes 1572872 | tf_op jit(solution)/shard_map/ppermute | solution.py:77
  457.2 12.7 %collective-permute-start.21 = (bf16[128,2048]{1,0:T(8,128)(2,1)}, bf16[128,2048]{1,0:T(8,128)(2,1)}, u32[]{:S(2)}, u32[]{:S(2)}) collective-permute-start(bf16[128,2048]{1,0:T(8,128)(2,1)} %get-tuple-element.69), channel_id=1, source_target_pairs={{0,3},{1,0},{2,1},{3,2},{4,7},{5,4},{6,5},{7,6},{8,11},{9,8},{10,9... | collective-permute-start | bytes 1572872 | tf_op jit(solution)/shard_map/ppermute | solution.py:77
  463.1 30.6 %collective-permute-start.20 = (bf16[128,2048]{1,0:T(8,128)(2,1)}, bf16[128,2048]{1,0:T(8,128)(2,1)S(1)}, u32[]{:S(2)}, u32[]{:S(2)}) collective-permute-start(bf16[128,2048]{1,0:T(8,128)(2,1)} %get-tuple-element.70), channel_id=1, source_target_pairs={{0,2},{1,3},{2,0},{3,1},{4,6},{5,7},{6,4},{7,5},{8,10},{9,11},{10,... | collective-permute-start | bytes 1572872 | tf_op jit(solution)/shard_map/ppermute | solution.py:77
  465.5 39.3 %collective-permute-start.19 = (bf16[128,2048]{1,0:T(8,128)(2,1)S(1)}, bf16[128,2048]{1,0:T(8,128)(2,1)S(1)}, u32[]{:S(2)}, u32[]{:S(2)}) collective-permute-start(bf16[128,2048]{1,0:T(8,128)(2,1)S(1)} %get-tuple-element.68), channel_id=1, source_target_pairs={{0,1},{1,2},{2,3},{3,0},{4,5},{5,6},{6,7},{7,4},{8,9},{9,10},{10,1... | collective-permute-start | bytes 1572872 | tf_op jit(solution)/shard_map/ppermute | solution.py:77
  466.4 94.7 %collective-permute-start.42 = (bf16[512,768]{0,1:T(8,128)(2,1)S(1)}, bf16[512,768]{0,1:T(8,128)(2,1)S(1)}, u32[]{:S(2)}, u32[]{:S(2)}) collective-permute-start(bf16[512,768]{0,1:T(8,128)(2,1)S(1)} %collective-permute-done.41), channel_id=1, source_target_pairs={{0,4},{4,0},{1,5},{5,1},{2,6},{6,2},{3,7},{7,3},{8,12},{12,8},{9,1... | collective-permute-start | bytes 2359304 | tf_op jit(solution)/shard_map/ppermute | solution.py:66
  507.3 5.1 collective-permute-start.34
  509.0 47.4 %collective-permute-start.22 = (bf16[128,2048]{1,0:T(8,128)(2,1)}, bf16[128,2048]{1,0:T(8,128)(2,1)S(1)}, u32[]{:S(2)}, u32[]{:S(2)}) collective-permute-start(bf16[128,2048]{1,0:T(8,128)(2,1)} %pad_maximum_fusion.13), channel_id=1, source_target_pairs={{0,1},{1,2},{2,3},{3,0},{4,5},{5,6},{6,7},{7,4},{8,9},{9,10},{10,1... | collective-permute-start | bytes 1572872 | tf_op jit(solution)/shard_map/ppermute | solution.py:77
  511.2 48.7 %collective-permute-start.23 = (bf16[128,2048]{1,0:T(8,128)(2,1)}, bf16[128,2048]{1,0:T(8,128)(2,1)S(1)}, u32[]{:S(2)}, u32[]{:S(2)}) collective-permute-start(bf16[128,2048]{1,0:T(8,128)(2,1)} %pad_maximum_fusion.13), channel_id=1, source_target_pairs={{0,2},{1,3},{2,0},{3,1},{4,6},{5,7},{6,4},{7,5},{8,10},{9,11},{10,... | collective-permute-start | bytes 1572872 | tf_op jit(solution)/shard_map/ppermute | solution.py:77
  511.2 58.4 %collective-permute-start.24 = (bf16[128,2048]{1,0:T(8,128)(2,1)}, bf16[128,2048]{1,0:T(8,128)(2,1)}, u32[]{:S(2)}, u32[]{:S(2)}) collective-permute-start(bf16[128,2048]{1,0:T(8,128)(2,1)} %pad_maximum_fusion.13), channel_id=1, source_target_pairs={{0,3},{1,0},{2,1},{3,2},{4,7},{5,4},{6,5},{7,6},{8,11},{9,8},{10,9... | collective-permute-start | bytes 1572872 | tf_op jit(solution)/shard_map/ppermute | solution.py:77
  512.4 2.3 collective-permute-start.35
  514.6 2.8 collective-permute-start.36
  516.2 45.2 %copy-start.18 = (f32[1,512,2048]{2,1,0:T(8,128)}, f32[1,512,2048]{2,1,0:T(8,128)S(1)}, u32[]{:S(2)}) copy-start(f32[1,512,2048]{2,1,0:T(8,128)S(1)} %convert_dynamic-update-slice_fusion.3) | copy-start | bytes 12582916
  517.4 26.8 %collective-permute-start.37 = (f32[2,512]{1,0:T(2,128)S(1)}, f32[2,512]{1,0:T(2,128)S(1)}, u32[]{:S(2)}, u32[]{:S(2)}) collective-permute-start(f32[2,512]{1,0:T(2,128)S(1)} %add.525), channel_id=1, source_target_pairs={{0,1},{1,0},{2,3},{3,2},{4,5},{5,4},{6,7},{7,6},{8,9},{9,8},{10,11... | collective-permute-start | bytes 12296 | tf_op jit(solution)/shard_map/ppermute | solution.py:352
  544.2 11.6 %collective-permute-start.38 = (f32[2,512]{1,0:T(2,128)S(1)}, f32[2,512]{1,0:T(2,128)S(1)}, u32[]{:S(2)}, u32[]{:S(2)}) collective-permute-start(f32[2,512]{1,0:T(2,128)S(1)} %add.526), channel_id=1, source_target_pairs={{0,2},{1,3},{2,0},{3,1},{4,6},{5,7},{6,4},{7,5},{8,10},{9,11},{10,... | collective-permute-start | bytes 12296 | tf_op jit(solution)/shard_map/ppermute | solution.py:352
  555.8 11.7 %collective-permute-start.31 = (bf16[128,2048]{1,0:T(8,128)(2,1)}, bf16[128,2048]{1,0:T(8,128)(2,1)}, u32[]{:S(2)}, u32[]{:S(2)}) collective-permute-start(bf16[128,2048]{1,0:T(8,128)(2,1)} %pad_maximum_fusion.14), channel_id=1, source_target_pairs={{0,1},{1,2},{2,3},{3,0},{4,5},{5,6},{6,7},{7,4},{8,9},{9,10},{10,1... | collective-permute-start | bytes 1572872 | tf_op jit(solution)/shard_map/ppermute | solution.py:77
  556.4 43.9 %collective-permute-start.32 = (bf16[128,2048]{1,0:T(8,128)(2,1)}, bf16[128,2048]{1,0:T(8,128)(2,1)}, u32[]{:S(2)}, u32[]{:S(2)}) collective-permute-start(bf16[128,2048]{1,0:T(8,128)(2,1)} %pad_maximum_fusion.14), channel_id=1, source_target_pairs={{0,2},{1,3},{2,0},{3,1},{4,6},{5,7},{6,4},{7,5},{8,10},{9,11},{10,... | collective-permute-start | bytes 1572872 | tf_op jit(solution)/shard_map/ppermute | solution.py:77
  559.9 45.8 %collective-permute-start.33 = (bf16[128,2048]{1,0:T(8,128)(2,1)}, bf16[128,2048]{1,0:T(8,128)(2,1)}, u32[]{:S(2)}, u32[]{:S(2)}) collective-permute-start(bf16[128,2048]{1,0:T(8,128)(2,1)} %pad_maximum_fusion.14), channel_id=1, source_target_pairs={{0,3},{1,0},{2,1},{3,2},{4,7},{5,4},{6,5},{7,6},{8,11},{9,8},{10,9... | collective-permute-start | bytes 1572872 | tf_op jit(solution)/shard_map/ppermute | solution.py:77
  (81 other events, 618.8 us)

commit v2 on v1

v2 whole, which is shorter than its diff:
```python
import math

import jax
import jax.numpy as jnp
from jax import lax
from jax.experimental import pallas as pl
from jax.experimental.pallas import tpu as pltpu
from jax.sharding import PartitionSpec as P

HD = 256
ROT = 64


NORM_EPSILON = 1e-05
MASK_FLOOR = -1000000000.0
F32 = jnp.float32
BF16 = jnp.bfloat16
LANES = 128
RELAY = {"attention": True, "fc1": True, "fc2": False}


def rotation_tables(position):
    half = ROT // 2
    frequency = jnp.exp(jnp.arange(half, dtype=F32) * (-2.0 * math.log(10000.0) / ROT))
    angles = position.astype(F32)[:, None] * frequency[None, :]
    cosine, sine = jnp.cos(angles), jnp.sin(angles)
    rest = (position.shape[0], LANES - ROT)
    return (
        jnp.concatenate([cosine, cosine, jnp.ones(rest, F32)], axis=1),
        jnp.concatenate([-sine, sine, jnp.zeros(rest, F32)], axis=1),
    )


def packed_rows(order_row, slots, block_rows):
    selector = slots[:, None] == jnp.arange(order_row.shape[0], dtype=jnp.int32)[None, :]
    source_block = jnp.sum(jnp.where(selector, order_row[None, :], 0), axis=1, dtype=jnp.int32)
    within = jnp.arange(block_rows, dtype=jnp.int32)
    return (source_block[:, None] * block_rows + within[None, :]).reshape(-1)


def place_rows(packed_at, lengths_row):
    seq_ends = jnp.cumsum(lengths_row, dtype=jnp.int32)
    passed = packed_at[:, None] >= seq_ends[None, :]
    segment = jnp.sum(passed.astype(jnp.int32), axis=1, dtype=jnp.int32)
    before = jnp.sum(jnp.where(passed, lengths_row[None, :], 0), axis=1, dtype=jnp.int32)
    return (segment, packed_at - before)


def dot(a, b, contract):
    return lax.dot_general(a, b, (contract, ((), ())), preferred_element_type=F32)


def fsdp_permute(x, bits):
    size, lanes = lax.axis_size("fsdp"), lax.axis_size("ctx")
    perm = [
        (f * lanes + x, (f ^ bits[x % 2]) * lanes + x) for f in range(size) for x in range(lanes)
    ]
    return lax.ppermute(x, ("fsdp", "ctx"), perm)


def swap(x, bit):
    return fsdp_permute(x, (bit, bit))


def ctx_pair(x):
    return lax.ppermute(x, "ctx", [(0, 1), (1, 0)])


def ctx_terms(x):
    if lax.axis_size("ctx") == 2:
        return x, ctx_pair(x)
    return lax.psum(x.astype(F32), "ctx"), jnp.zeros_like(x)


def tp_pair(x, bit):
    return lax.ppermute(x, "tp", [(i, i ^ bit) for i in range(lax.axis_size("tp"))])


def half_of(x, which, axis):
    size = x.shape[axis] // 2
    return lax.dynamic_slice_in_dim(x, which * size, size, axis=axis)


def kernel_call(body, scalars, arrays, in_specs, out_shape, out_specs, grid, name, flops=0, scratch=()):
    outs = out_shape if isinstance(out_shape, (tuple, list)) else (out_shape,)
    size = sum(a.size * a.dtype.itemsize for a in (*arrays, *outs))
    return pl.pallas_call(
        body,
        out_shape=out_shape,
        grid_spec=pltpu.PrefetchScalarGridSpec(
            num_scalar_prefetch=1,
            grid=grid,
            in_specs=in_specs,
            out_specs=out_specs,
            scratch_shapes=scratch,
        ),
        cost_estimate=pl.CostEstimate(flops=flops, transcendentals=0, bytes_accessed=size),
        name=name,
    )(scalars, *arrays)


def aligned(index, size):
    return pl.ds(pl.multiple_of(index * size, size), size)


def frame_rows(own, other, order, norm=None):
    rows, columns = own.shape
    width, step = columns // 4, rows // 2

    def kernel(order_ref, own_ref, other_ref, *refs):
        gain_ref, bias_ref, out_ref, wide_ref = refs if norm else (None, None, refs[0], None)
        for s, ref in enumerate((own_ref, other_ref)):
            if norm:
                x = ref[...].astype(F32)
                x = x - jnp.mean(x, axis=1, keepdims=True)
                variance = jnp.mean(x * x, axis=1, keepdims=True)
                wide_ref[...] = x * lax.rsqrt(variance + NORM_EPSILON)
            for k in range(4):
                to = slice(k * width, (k + 1) * width)
                at = aligned(order_ref[k], width)
                if norm:
                    out_ref[s, :, to] = (
                        wide_ref[:, at] * gain_ref[:, to] + bias_ref[:, to]
                    ).astype(BF16)
                else:
                    out_ref[s, :, to] = ref[:, at]

    row_spec = pl.BlockSpec((step, columns), lambda r, o: (r, 0))
    vector_spec = pl.BlockSpec((1, columns), lambda r, o: (0, 0))
    out = kernel_call(
        kernel,
        order,
        (own, other, *(norm or ())),
        [row_spec, row_spec] + ([vector_spec, vector_spec] if norm else []),
        jax.ShapeDtypeStruct((2, rows, columns), BF16),
        pl.BlockSpec((2, step, columns), lambda r, o: (0, r, 0)),
        (2,),
        "norm_rows" if norm else "frame_rows",
        scratch=[pltpu.VMEM((step, columns), F32)] if norm else (),
    )
    return out.reshape(2 * rows, columns)


def place_grad(parts, core, attention):
    rows, columns = parts[0].shape
    step = rows // 2

    def kernel(core_ref, a_ref, ax_ref, b_ref, bx_ref, *out_refs):
        for h, (u_ref, ux_ref) in enumerate(((a_ref, ax_ref), (b_ref, bx_ref))):
            total = u_ref[...].astype(F32) + ux_ref[...].astype(F32)
            place = core_ref[0] ^ h
            if attention:
                for t in range(3):
                    out_refs[0][t, :, aligned(place, HD)] = total[:, t * HD : (t + 1) * HD]
                out_refs[1][:, aligned(place, HD)] = total[:, 3 * HD :]
            else:
                out_refs[0][:, aligned(place, columns)] = total

    shapes = [(rows, 2 * columns)]
    specs = [pl.BlockSpec((step, 2 * columns), lambda r, c: (r, 0))]
    if attention:
        shapes = [(3, rows, 2 * HD), (rows, 2 * HD)]
        specs = [
            pl.BlockSpec((3, step, 2 * HD), lambda r, c: (0, r, 0)),
            pl.BlockSpec((step, 2 * HD), lambda r, c: (r, 0)),
        ]
    return kernel_call(
        kernel,
        core[None],
        parts,
        [pl.BlockSpec((step, columns), lambda r, c: (r, 0))] * 4,
        [jax.ShapeDtypeStruct(shape, F32) for shape in shapes],
        specs,
        (2,),
        "place_grad",
    )


def share_rows(first, second, rows, theirs=None):
    width = first[1][0].shape[0]
    at = 1 if theirs is None else 0

    def kernel(_, f_ref, s_ref, *refs):
        f_refs, s_refs, refs = refs[:4], refs[4:8], refs[8:]
        for n in range(2):

            @pl.when(pl.program_id(0) == n)
            def _(n=n):
                for m in range(2):
                    k = 2 * n + m
                    total = dot(f_ref[...], f_refs[k][...], ((1,), (1,)))
                    total = total + dot(s_ref[...], s_refs[k][...], ((1,), (1,)))
                    if theirs is None:
                        to = slice((1 - m) * width, (2 - m) * width)
                    else:
                        to = slice(m * width, (m + 1) * width)
                        total = total + refs[0][:, to].astype(F32)
                    refs[-1][:, to] = total.astype(BF16)

    arrays, in_specs, flops = [], [], 0
    for acts, _, _, size in (first, second):
        arrays.append(acts)
        in_specs.append(pl.BlockSpec((rows, size), lambda n, b: (at, 0)))
        flops += 2 * rows * 4 * width * size
    for _, pieces, block, size in (first, second):
        arrays += pieces
        in_specs += [pl.BlockSpec((width, size), lambda n, b, block=block: (0, block))] * 4
    out_spec = pl.BlockSpec((rows, 2 * width), lambda n, b: (0, n))
    if theirs is not None:
        arrays.append(theirs)
        in_specs.append(out_spec)
    return kernel_call(
        kernel,
        jnp.zeros((1,), jnp.int32),
        arrays,
        in_specs,
        jax.ShapeDtypeStruct((rows, 4 * width), BF16),
        out_spec,
        (2,),
        "share_rows",
        flops=flops,
    )


def finish_output(order, row_block, kept, got, inputs, out_bias):
    rows, columns = kept.shape
    width = columns // 4

    def kernel(s_ref, kept_ref, got_ref, x_ref, bias_ref, out_ref):
        for k in range(4):
            cols, at = slice(k * width, (k + 1) * width), aligned(s_ref[k], width)
            total = kept_ref[:, cols] + got_ref[:, cols].astype(F32)
            out_ref[:, at] = (x_ref[:, at].astype(F32) + total + bias_ref[:, cols]).astype(BF16)

    spec = pl.BlockSpec((rows, columns), lambda i, s: (0, 0))
    return kernel_call(
        kernel,
        jnp.concatenate([order, row_block[None]]),
        (kept, got, inputs, out_bias),
        [
            spec,
            spec,
            pl.BlockSpec((rows, columns), lambda i, s: (s[4], 0)),
            pl.BlockSpec((1, columns), lambda i, s: (0, 0)),
        ],
        jax.ShapeDtypeStruct((rows, columns), BF16),
        spec,
        (1,),
        "finish_output",
    )


def finish_input_grad(order, row_block, kept, got, inputs, upstream, norm_gain):
    rows, columns = kept.shape
    width = columns // 4

    def kernel(s_ref, kept_ref, got_ref, x_ref, dy_ref, gain_ref, out_ref, std_ref):
        x = x_ref[...].astype(F32)
        x = x - jnp.mean(x, axis=1, keepdims=True)
        inverse = lax.rsqrt(jnp.mean(x * x, axis=1, keepdims=True) + NORM_EPSILON)
        std_ref[...] = x * inverse
        mean_scaled = jnp.zeros((rows, 1), F32)
        mean_product = jnp.zeros((rows, 1), F32)

        def parts(k):
            cols, at = slice(k * width, (k + 1) * width), aligned(s_ref[k], width)
            total = kept_ref[:, cols] + got_ref[:, cols].astype(F32)
            return at, total * gain_ref[:, cols], std_ref[:, at]

        for k in range(4):
            _, scaled, standard = parts(k)
            mean_scaled += jnp.sum(scaled, axis=1, keepdims=True) / columns
            mean_product += jnp.sum(scaled * standard, axis=1, keepdims=True) / columns
        for k in range(4):
            at, scaled, standard = parts(k)
            change = inverse * (scaled - mean_scaled - standard * mean_product)
            out_ref[:, at] = (dy_ref[:, at].astype(F32) + change).astype(BF16)

    spec = pl.BlockSpec((rows, columns), lambda i, s: (0, 0))
    rows_spec = pl.BlockSpec((rows, columns), lambda i, s: (s[4], 0))
    return kernel_call(
        kernel,
        jnp.concatenate([order, row_block[None]]),
        (kept, got, inputs, upstream, norm_gain),
        [spec, spec, rows_spec, rows_spec, pl.BlockSpec((1, columns), lambda i, s: (0, 0))],
        jax.ShapeDtypeStruct((rows, columns), BF16),
        spec,
        (1,),
        "finish_input_grad",
        scratch=[pltpu.VMEM((rows, columns), F32)],
    )


def norm_grads(order, inputs, share):
    rows, columns = inputs.shape
    width, step = columns // 4, rows // 2

    def kernel(order_ref, x_ref, share_ref, out_ref, std_ref):
        @pl.when(pl.program_id(0) == 0)
        def _():
            out_ref[...] = jnp.zeros_like(out_ref)

        x = x_ref[...].astype(F32)
        x = x - jnp.mean(x, axis=1, keepdims=True)
        std_ref[...] = x * lax.rsqrt(jnp.mean(x * x, axis=1, keepdims=True) + NORM_EPSILON)
        for k in range(4):
            cols = slice(k * width, (k + 1) * width)
            part = share_ref[:, cols].astype(F32)
            product = part * std_ref[:, aligned(order_ref[k], width)]
            out_ref[0:1, cols] += jnp.sum(product, axis=0, keepdims=True)
            out_ref[1:2, cols] += jnp.sum(part, axis=0, keepdims=True)

    row_spec = pl.BlockSpec((step, columns), lambda r, o: (r, 0))
    return kernel_call(
        kernel,
        order,
        (inputs, share),
        [row_spec, row_spec],
        jax.ShapeDtypeStruct((2, columns), F32),
        pl.BlockSpec((2, columns), lambda r, o: (0, 0)),
        (2,),
        "norm_grads",
        scratch=[pltpu.VMEM((step, columns), F32)],
    )


def gather_rows(pieces, places, dtype):
    size, (rows, columns) = len(pieces), pieces[0].shape

    def kernel(place_ref, *refs):
        for n in range(size):
            refs[-1][aligned(place_ref[n], rows), :] = refs[n][...].astype(dtype)

    return kernel_call(
        kernel,
        places,
        pieces,
        [pl.BlockSpec((rows, columns // 2), lambda c, p: (0, c))] * size,
        jax.ShapeDtypeStruct((rows * size, columns), dtype),
        pl.BlockSpec((rows * size, columns // 2), lambda c, p: (0, c)),
        (2,),
        "gather_rows",
    )


def turned(x, cosine, sine):
    lane = lax.broadcasted_iota(jnp.int32, x.shape, 1)
    half = ROT // 2
    partner = jnp.where(
        lane < half, pltpu.roll(x, x.shape[1] - half, axis=1), pltpu.roll(x, half, axis=1)
    )
    return x * cosine + partner * sine


def project(normed, pieces, bias, cosine, sine):
    rows = normed.shape[0] // 2
    width = pieces[0].shape[0]

    def kernel(_, x_ref, *refs):
        piece_refs, (bias_ref, cos_ref, sin_ref, q_ref, kv_ref) = refs[:4], refs[4:]
        total = dot(x_ref[:, :width], piece_refs[0][...], ((1,), (0,)))
        for k in range(1, 4):
            cols = slice(k * width, (k + 1) * width)
            total = total + dot(x_ref[:, cols], piece_refs[k][...], ((1,), (0,)))
        total = total + bias_ref[...]
        cosine, sine = cos_ref[...], sin_ref[...]
        for n, ref in enumerate((q_ref, kv_ref)):
            head = total[:, n * HD : (n + 1) * HD]
            ref[:, :LANES] = turned(head[:, :LANES], cosine, sine).astype(BF16)
            ref[:, LANES:HD] = head[:, LANES:].astype(BF16)
        kv_ref[:, HD:] = total[:, 2 * HD :].astype(BF16)

    def by_row(columns):
        return pl.BlockSpec((rows, columns), lambda s, z: (s, 0))

    return kernel_call(
        kernel,
        jnp.zeros((1,), jnp.int32),
        (normed, *pieces, bias, cosine, sine),
        [by_row(normed.shape[1])]
        + [pl.BlockSpec((width, 3 * HD), lambda s, z: (0, 0))] * 4
        + [pl.BlockSpec((1, 3 * HD), lambda s, z: (0, 0)), by_row(LANES), by_row(LANES)],
        [
            jax.ShapeDtypeStruct((2 * rows, HD), BF16),
            jax.ShapeDtypeStruct((2 * rows, 2 * HD), BF16),
        ],
        [by_row(HD), by_row(2 * HD)],
        (2,),
        "project",
        flops=2 * 2 * rows * normed.shape[1] * 3 * HD,
    )


def turn_back(query_grad, kept, got, cosine, sine):
    rows = kept.shape[1]

    def kernel(_, q_ref, kept_ref, got_ref, cos_ref, sin_ref, out_ref):
        both = kept_ref[...] + got_ref[...].astype(F32)
        cosine, sine = cos_ref[...], -sin_ref[...]
        for n, head in enumerate((q_ref[...], both[:, :HD])):
            at = n * HD
            out_ref[:, at : at + LANES] = turned(head[:, :LANES], cosine, sine).astype(BF16)
            out_ref[:, at + LANES : at + HD] = head[:, LANES:].astype(BF16)
        out_ref[:, 2 * HD :] = both[:, HD:].astype(BF16)

    def by_row(columns):
        return pl.BlockSpec((rows, columns), lambda s, z: (s, 0))

    both_spec = pl.BlockSpec((None, rows, 2 * HD), lambda s, z: (s, 0, 0))
    return kernel_call(
        kernel,
        jnp.zeros((1,), jnp.int32),
        (query_grad, kept, got, cosine, sine),
        [by_row(HD), both_spec, both_spec, by_row(LANES), by_row(LANES)],
        jax.ShapeDtypeStruct((2 * rows, 3 * HD), BF16),
        by_row(3 * HD),
        (2,),
        "turn_back",
    )


def attended_grads(upstream, pieces, valid):
    rows = upstream.shape[0] // 2
    width = pieces[0].shape[0]

    def kernel(_, dy_ref, *refs):
        piece_refs, (valid_ref, out_ref) = refs[:4], refs[4:]
        total = dot(dy_ref[:, :width], piece_refs[0][...], ((1,), (0,)))
        for k in range(1, 4):
            cols = slice(k * width, (k + 1) * width)
            total = total + dot(dy_ref[:, cols], piece_refs[k][...], ((1,), (0,)))
        out_ref[...] = total.astype(BF16) * valid_ref[...].astype(BF16)

    def by_row(columns):
        return pl.BlockSpec((rows, columns), lambda s, z: (s, 0))

    return kernel_call(
        kernel,
        jnp.zeros((1,), jnp.int32),
        (upstream, *pieces, valid),
        [by_row(upstream.shape[1])]
        + [pl.BlockSpec((width, HD), lambda s, z: (0, 3))] * 4
        + [by_row(1)],
        jax.ShapeDtypeStruct((2 * rows, HD), BF16),
        by_row(HD),
        (2,),
        "attended_grads",
        flops=2 * 2 * rows * upstream.shape[1] * HD,
    )


def pack_attention(qkv_weight, dense_weight, halves):
    rows = qkv_weight.shape[1]
    count = halves.shape[0]

    def kernel(h_ref, qkv_ref, dense_ref, *out_refs):
        for n in range(count):
            for t in range(3):
                out_refs[n][:, t * HD : (t + 1) * HD] = qkv_ref[t, :, aligned(h_ref[n], HD)]
            out_refs[n][:, 3 * HD :] = dense_ref[:, aligned(h_ref[n], HD)]

    def spec(columns):
        return pl.BlockSpec((rows // 2, columns), lambda r, h: (r, 0))

    return kernel_call(
        kernel,
        halves,
        (qkv_weight, dense_weight),
        [pl.BlockSpec((3, rows // 2, 2 * HD), lambda r, h: (0, r, 0)), spec(2 * HD)],
        [jax.ShapeDtypeStruct((rows, 4 * HD), BF16)] * count,
        [spec(4 * HD)] * count,
        (2,),
        "pack_attention",
    )


class Rounds:
    def __init__(self):
        self.last = ()

    def __call__(self, *arrays):
        got = lax.optimization_barrier((*arrays, *self.last))[: len(arrays)]
        return got if len(arrays) > 1 else got[0]

    def done(self, *arrays):
        self.last = arrays
        return arrays if len(arrays) > 1 else arrays[0]

    def close(self, *arrays):
        self.last = (*self.last, *arrays)


def per_device(
    tokens,
    lengths,
    block_order,
    ln_gain,
    ln_bias,
    qkv_weight,
    qkv_bias,
    dense_weight,
    dense_bias,
    fc1_weight,
    fc1_bias,
    fc2_weight,
    fc2_bias,
    cotangent,
):
    me = lax.axis_index("fsdp")
    core = me % 2
    tp_index = lax.axis_index("tp").astype(jnp.int32)
    tp_size = lax.axis_size("tp")
    ctx_index = lax.axis_index("ctx")
    ctx_size = lax.axis_size("ctx")
    pairs = ctx_size == 2
    side = ctx_index % 2 if pairs else 0 * ctx_index
    shard = ln_gain.shape[0]
    row_count = tokens.shape[1]
    block_rows = row_count // 2
    score_scale = 1.0 / math.sqrt(HD)
    order = jnp.stack([me, me ^ 1, me ^ (2 + side), me ^ (3 - side)]).astype(jnp.int32)
    near_bits, far_bits = ((2, 3), (3, 2)) if pairs else ((2, 2), (3, 3))
    inputs_low, upstream_low = tokens[0], cotangent[0]
    then = Rounds()

    halves = jnp.stack([core, 1 - core, core ^ side, core ^ 1 ^ side]).astype(jnp.int32)

    def relayed(name):
        return RELAY[name] and pairs

    def four(weight, name):
        return [half_of(weight, halves[n], 1) for n in range(3 if relayed(name) else 4)]

    def far_of(name, near, packs):
        return ctx_pair(near) if relayed(name) else fsdp_permute(then(packs[3]), far_bits)

    def joined(pieces):
        return jnp.concatenate(pieces, axis=0)

    seq_count, slots = lengths.shape[1], block_order.shape[1]
    vectors = jnp.concatenate(
        [
            v.astype(F32)
            for v in (ln_gain, ln_bias, dense_bias, fc2_bias, lengths[0], block_order[0])
        ]
    )
    then.done(vectors)
    vectors = [
        vectors,
        swap(vectors, 1),
        fsdp_permute(vectors, near_bits),
        fsdp_permute(vectors, far_bits),
    ]
    inputs_other = swap(inputs_low, 1)
    fc1_packs = four(then(fc1_weight), "fc1")
    then.done(*fc1_packs)
    fc1_near = fsdp_permute(fc1_packs[2], near_bits)
    packs = pack_attention(
        qkv_weight.transpose(1, 0, 2), then(dense_weight), halves[: 3 if relayed("attention") else 4]
    )
    then.done(*packs)
    then.close(inputs_other, *vectors[1:])

    def over_features(n):
        return jnp.concatenate([v[n * shard : (n + 1) * shard] for v in vectors])[None, :]

    norm_gain, norm_bias = over_features(0), over_features(1)
    out_bias = over_features(2) + over_features(3)
    their_layout = vectors[1][4 * shard :].astype(jnp.int32)

    upstream_other = swap(then(upstream_low), 1)
    fc1_core, attention_core = swap(then(fc1_packs[1]), 1), swap(then(packs[1]), 1)
    normed = then.done(frame_rows(inputs_low, then(inputs_other), order, (norm_gain, norm_bias)))
    fc2_packs = four(then(fc2_weight), "fc2")
    then.done(*fc2_packs)
    layouts = [
        (then(lengths[0]), block_order[0]),
        (their_layout[:seq_count], their_layout[seq_count:]),
    ]
    local_slots = ctx_index * 2 + jnp.arange(2, dtype=jnp.int32)
    if pairs:
        key_slots = jnp.concatenate([local_slots, (1 - ctx_index) * 2 + jnp.arange(2)])
    else:
        key_slots = jnp.arange(slots, dtype=jnp.int32)
    allowed, valid, positions = [], [], []
    for lengths_row, order_row in layouts:
        local_packed = packed_rows(order_row, local_slots, block_rows)
        key_packed = packed_rows(order_row, key_slots, block_rows)
        segment, position = place_rows(local_packed, lengths_row)
        key_segment = place_rows(key_packed, lengths_row)[0]
        allowed.append(
            (segment[:, None] == key_segment[None, :])
            & (key_packed[None, :] <= local_packed[:, None])
        )
        valid.append((segment < seq_count).astype(F32)[:, None])
        positions.append(position)
    cosine_table, sine_table = rotation_tables(jnp.concatenate(positions))
    valid = jnp.concatenate(valid)
    upstream_sum = jnp.sum(upstream_low.astype(F32), axis=0, keepdims=True)
    then.done(cosine_table, sine_table, valid, upstream_sum, *fc2_packs)
    then.close(upstream_other, fc1_core, attention_core, fc1_near)

    attention_near = fsdp_permute(then(packs[2]), near_bits)
    fc1_far = far_of("fc1", then(fc1_near), fc1_packs)
    fc2_core = swap(then(fc2_packs[1]), 1)
    upstream = then.done(frame_rows(upstream_low, then(upstream_other), order))
    fc1_pieces = [fc1_packs[0], fc1_core, fc1_near, fc1_far]
    then.close(attention_near, fc1_far, fc2_core)

    def grad_block(k, *products, kind=BF16):
        parts = []
        for left, right in products:
            rows = lax.dynamic_slice_in_dim(left, k * shard, shard, axis=1)
            parts.append(dot(rows, right, ((0,), (0,))).astype(kind))
        return jnp.concatenate(parts, axis=1)

    def grad_blocks(*products):
        far = grad_block(2 + side, *products)
        rest = [grad_block(k, *products) for k in (3 - side, 1)]
        return (far, *rest, grad_block(0, *products, kind=F32))

    def add_mine(own, far):
        return then.done((own + then(far).astype(F32)).astype(BF16))

    def add_theirs(near, farther):
        return then.done((near.astype(F32) + then(farther).astype(F32)).astype(BF16))

    def placed(mine, theirs, attention=False):
        parts = then(*mine, *theirs)
        return then.done(*place_grad(parts, core, attention))

    fc2_near = fsdp_permute(then(fc2_packs[2]), near_bits)
    attention_far = far_of("attention", then(attention_near), packs)
    attention = [packs[0], attention_core, attention_near, attention_far]
    pre_act = dot(then(normed), joined(fc1_pieces), ((1,), (0,)))
    pre_act = pre_act + half_of(fc1_bias, core, 0).astype(F32)[None, :]
    normal_cdf = 0.5 * (1.0 + lax.erf(pre_act * (1.0 / math.sqrt(2.0))))
    density = jnp.exp(-0.5 * pre_act * pre_act) * (1.0 / math.sqrt(2.0 * math.pi))
    hidden = (pre_act * normal_cdf).astype(BF16)
    slope = normal_cdf + pre_act * density
    hidden, slope = then.done(hidden, slope)
    fc2_blocks = then.done(*grad_blocks((then(upstream), hidden)))
    then.close(fc2_near, attention_far)

    fc2_far = far_of("fc2", then(fc2_near), fc2_packs)
    fc2_pieces = [fc2_packs[0], fc2_core, fc2_near, fc2_far]
    fc2_grad_near = swap(then(fc2_blocks[2]), 1)
    qkv_bias_own = half_of(qkv_bias, core, 1).astype(F32).reshape(1, 3 * HD)
    queries, both_local = then.done(
        *project(then(normed), attention, qkv_bias_own, cosine_table, sine_table)
    )
    both_local = both_local.reshape(2, row_count, 2 * HD)
    if pairs:
        both_other = ctx_pair(both_local)
    else:
        both_other = lax.all_gather(both_local, "ctx", axis=1, tiled=True)
    attended_grad = then.done(attended_grads(then(upstream), attention, valid))
    then.close(both_other, fc2_far, fc2_grad_near)
    both_all = then(both_other)
    if pairs:
        both_all = jnp.concatenate([both_local, both_all], axis=1)

    fc2_grad_far = swap(then(fc2_blocks[0]), 2)
    attended, probs_all = [], []
    for s in range(2):
        rows = slice(s * row_count, (s + 1) * row_count)
        keys, values = both_all[s, :, :HD], both_all[s, :, HD:]
        scores = dot(queries[rows], keys, ((1,), (1,))) * score_scale
        scores = jnp.where(allowed[s], scores, MASK_FLOOR)
        exp_scores = jnp.exp(scores - jnp.max(scores, axis=1, keepdims=True))
        probs = exp_scores / jnp.sum(exp_scores, axis=1, keepdims=True)
        probs_all.append(probs)
        attended.append(dot(probs.astype(BF16), values, ((1,), (0,))))
    attended = then.done((jnp.concatenate(attended) * valid).astype(BF16))
    hidden_size = hidden.shape[1]
    second = (hidden, fc2_pieces, 0, hidden_size)
    theirs = then.done(share_rows((attended, attention, 3, HD), second, row_count))
    hidden_grad = dot(then(upstream), joined(fc2_pieces), ((1,), (0,)))
    pre_grad = then.done((hidden_grad * slope).astype(BF16))
    then.close(fc2_grad_far, theirs)

    def attention_grads(s):
        rows = slice(s * row_count, (s + 1) * row_count)
        keys, values = both_all[s, :, :HD], both_all[s, :, HD:]
        probs, head_grad = probs_all[s], then(attended_grad[rows])
        prob_grad = dot(head_grad, values, ((1,), (1,)))
        row_delta = jnp.sum(probs * prob_grad, axis=1, keepdims=True)
        score_grad = (probs * (prob_grad - row_delta)).astype(BF16)
        query_piece = dot(score_grad, keys, ((1,), (0,))) * score_scale
        key_piece = dot(score_grad, queries[rows], ((0,), (0,))) * score_scale
        value_piece = dot(probs.astype(BF16), head_grad, ((0,), (0,)))
        return then.done(query_piece, jnp.concatenate([key_piece, value_piece], axis=1))

    low = tp_index % 2

    def halves(total, digit):
        return then.done(
            half_of(total, 1 - digit, 0).astype(BF16), half_of(total, digit, 0).astype(F32)
        )

    def halve_on(kept, got, bit, row_block):
        while bit < tp_size:
            total, digit = kept + got.astype(F32), (tp_index // bit) % 2
            given, kept = halves(total, digit)
            got, row_block, bit = tp_pair(given, bit), row_block * 2 + digit, bit * 2
        return kept, got, row_block

    def double_up(part):
        pieces, flips, bit = [part], [0], tp_size // 2
        while bit > 1:
            pieces += [tp_pair(p, bit) for p in pieces]
            flips += [f ^ bit for f in flips]
            bit //= 2
        return pieces, flips + [f ^ 1 for f in flips]

    fc2_grad_farther = swap(then(fc2_blocks[1]), 3)
    theirs = swap(then(theirs), 1)
    fc2_mine = ctx_terms(add_mine(fc2_blocks[3], fc2_grad_far))
    grads_first = attention_grads(0)
    first = (then(attended), attention, 3, HD)
    shared = then.done(share_rows(first, second, row_count, theirs))
    given, kept = halves(shared, low)
    fc1_far_block = then.done(grad_block(2 + side, (then(normed), pre_grad)))
    then.close(fc2_grad_farther)

    fc1_grad_far = swap(then(fc1_far_block), 2)
    out_got = tp_pair(then(given), 1)
    grads_second = attention_grads(1)
    both_grad = jnp.stack([grads_first[1], grads_second[1]])
    query_grad = jnp.concatenate([grads_first[0], grads_second[0]])
    if pairs:
        both_given = both_grad[:, row_count:].astype(BF16)
        both_grad = both_grad[:, :row_count]
    else:
        both_given = jnp.zeros((2, row_count, 2 * HD), BF16)
        both_grad = lax.psum_scatter(both_grad, "ctx", scatter_dimension=1, tiled=True)
    both_given, both_grad, query_grad = then.done(both_given, both_grad, query_grad)
    both_got = ctx_pair(both_given) if pairs else both_given
    fc1_near_block = then.done(grad_block(1, (then(normed), pre_grad)))
    fc1_grad_near = swap(fc1_near_block, 1)
    fc1_rest = then.done(
        grad_block(3 - side, (then(normed), pre_grad)),
        grad_block(0, (then(normed), pre_grad), kind=F32),
    )
    then.close(fc1_grad_far, out_got, fc2_mine[1], fc1_grad_near)

    fc1_grad_farther = swap(then(fc1_rest[0]), 3)
    out_kept, out_got, out_block = halve_on(then(kept), out_got, 2, low)
    fc2_theirs = ctx_terms(add_theirs(fc2_grad_near, fc2_grad_farther))
    proj_grad = then.done(
        turn_back(then(query_grad), both_grad, both_got, cosine_table, sine_table)
    )
    second = (pre_grad, fc1_pieces, 0, hidden_size)
    theirs = then.done(share_rows((proj_grad, attention, 0, 3 * HD), second, row_count))
    products = (proj_grad, attended)

    def attention_block(k, kind=BF16):
        return grad_block(k, (then(normed), products[0]), (upstream, products[1]), kind=kind)

    far_block = then.done(attention_block(2 + side))
    then.close(fc1_grad_farther, out_got)

    attention_grad_far = swap(then(far_block), 2)
    theirs = swap(then(theirs), 1)
    out_part = then.done(
        finish_output(order, out_block, then(out_kept), out_got, inputs_low, out_bias)
    )
    out_pieces, flips = double_up(out_part)
    out_late = [tp_pair(out_part, 1)]
    near_block = then.done(attention_block(1))
    first = (then(proj_grad), attention, 0, 3 * HD)
    shared = then.done(share_rows(first, second, row_count, theirs))
    attention_grad_near = swap(near_block, 1)
    given, kept = halves(shared, low)
    fc1_mine = then.done((then(fc1_rest[1], fc2_theirs[1])[0] + fc1_grad_far).astype(BF16))
    fc1_mine = ctx_terms(fc1_mine)
    farther_block = then.done(attention_block(3 - side))
    then.close(attention_grad_far, out_late[0], *out_pieces[1:], attention_grad_near)

    attention_grad_farther = swap(then(farther_block), 3)
    got = tp_pair(then(given), 1)
    norm_sums = then.done(norm_grads(order, then(inputs_low), shared))
    own_block = then.done(attention_block(0, kind=F32))
    column_sums = then.done(
        jnp.concatenate(
            [jnp.sum(then(pre_grad).astype(F32), axis=0), jnp.sum(proj_grad.astype(F32), axis=0)]
        )
    )
    fc1_theirs = add_theirs(fc1_grad_near, fc1_grad_farther)
    fc1_theirs = ctx_terms(then(fc1_theirs, fc1_mine[1])[0])
    then.close(attention_grad_farther, got)

    kept, got, row_block = halve_on(then(kept), got, 2, low)
    out_late += [tp_pair(p, 1) for p in out_pieces[1:]]
    norm_sums = then(norm_sums)
    norm_sums = norm_sums + tp_pair(norm_sums, 1)
    fc2_out = placed(fc2_mine, fc2_theirs)
    attention_mine = add_mine(own_block, attention_grad_far)
    attention_mine = ctx_terms(then(attention_mine, fc1_theirs[1])[0])
    then.close(got, norm_sums)

    input_part = then.done(
        finish_input_grad(order, row_block, then(kept), got, inputs_low, upstream_low, norm_gain)
    )
    pieces, _ = double_up(input_part)
    late = [tp_pair(input_part, 1)]
    bit = 2
    while bit < tp_size:
        norm_sums = norm_sums + tp_pair(then(norm_sums), bit)
        bit *= 2
    vector_sums = jnp.concatenate([norm_sums[:, k * shard : (k + 1) * shard] for k in range(4)])

    def sums_of(k):
        return [
            lax.dynamic_slice_in_dim(vector_sums, 2 * k, 2, axis=0).reshape(-1),
            lax.dynamic_slice_in_dim(upstream_sum[0], order[k] * shard, shard),
        ]

    sums_kept = jnp.concatenate([*sums_of(0), *sums_of(1), column_sums])
    sums_given = jnp.concatenate([*sums_of(2 + side), *sums_of(3 - side), column_sums])
    sums_kept = sums_kept + swap(sums_given, 2)
    fc1_out = placed(fc1_mine, fc1_theirs)
    attention_theirs = add_theirs(attention_grad_near, attention_grad_farther)
    attention_theirs = ctx_terms(then(attention_theirs, attention_mine[1])[0])
    then.close(*pieces[1:], late[0], sums_kept)

    late += [tp_pair(p, 1) for p in then(*pieces, *out_late)[1 : len(pieces)]]
    sums_kept = sum(ctx_terms(then(sums_kept)))
    other_core = swap(sums_kept[3 * shard :], 1)
    vector_sums = (sums_kept[: 3 * shard] + other_core[: 3 * shard]).reshape(3, shard)
    column_sums, column_other = sums_kept[6 * shard :], other_core[3 * shard :]

    def row_block_of(index):
        place, bit = 0 * index, 1
        while bit < tp_size:
            place = place * 2 + (index // bit) % 2
            bit *= 2
        return place

    places = jnp.stack([row_block_of(tp_index ^ f) for f in flips]).astype(jnp.int32)
    output = then.done(gather_rows(then(*out_pieces, *out_late), places, BF16))
    input_grad = then.done(gather_rows(then(*pieces, *late), places, F32))
    qkv_out, dense_out = placed(attention_mine, attention_theirs, True)

    def in_order(mine, other, axis):
        return jnp.where(
            core == 0,
            jnp.concatenate([mine, other], axis=axis),
            jnp.concatenate([other, mine], axis=axis),
        )

    hidden_half = fc1_bias.shape[0] // 2
    fc1_bias_grad = in_order(column_sums[:hidden_half], column_other[:hidden_half], 0)
    qkv_bias_grad = in_order(
        column_sums[hidden_half:].reshape(3, HD), column_other[hidden_half:].reshape(3, HD), 1
    )
    return (
        output[None],
        input_grad[None],
        vector_sums[0],
        vector_sums[1],
        qkv_out.transpose(1, 0, 2),
        qkv_bias_grad,
        dense_out,
        vector_sums[2],
        fc1_out,
        fc1_bias_grad,
        fc2_out,
        vector_sums[2],
    )


def solution(mesh):
    placed = (
        P("fsdp", "ctx", None),
        P("fsdp", None),
        P("fsdp", None),
        P("fsdp"),
        P("fsdp"),
        P("fsdp", None, "tp"),
        P(None, "tp"),
        P("fsdp", "tp"),
        P("fsdp"),
        P("fsdp", "tp"),
        P("tp"),
        P("fsdp", "tp"),
        P("fsdp"),
        P("fsdp", "ctx", None),
    )
    return jax.shard_map(
        per_device,
        mesh=mesh,
        in_specs=placed,
        out_specs=(
            P("fsdp", "ctx", None),
            P("fsdp", "ctx", None),
            P("fsdp"),
            P("fsdp"),
            P("fsdp", None, "tp"),
            P(None, "tp"),
            P("fsdp", "tp"),
            P("fsdp"),
            P("fsdp", "tp"),
            P("tp"),
            P("fsdp", "tp"),
            P("fsdp"),
        ),
        check_vma=False,
    )
```

time: 615 us -> 439 us (0.71)
  the two profiles are of different devices: /device:TPU:9 before, /device:TPU:0 now
where the time goes in v2:
time: 439 us; the launch traced here: 431 us
  waiting for transfers between devices  144 us (33%)
  Pallas kernels  95.1 us (22%)
  matrix products  68.1 us (16%)
  other arithmetic  50.7 us (12%)
  starting transfers between devices  44.3 us (10%)
  local copies, waits for them, and re-layouts  25.1 us (6%)
    pallas_call x18, Pallas kernels, kernel_call(): pl.pallas_call(body, out_shape=out_shape, grid_spec=pltpu.PrefetchScalarG...  95.1 us
    dot_general x30, matrix products, dot(): lax.dot_general(a, b, (contract, ((), ())), preferred_element_type=F32)  68.1 us
    ppermute x11, waiting for transfers between devices, ctx_pair(): return lax.ppermute(x, 'ctx', [(0, 1), (1, 0)])  61.3 us
    ppermute x12, waiting for transfers between devices, tp_pair(): lax.ppermute(x, 'tp', [(i, i ^ bit) for i in range(lax.axis_size('tp'))])  47.7 us
    ppermute x25, waiting for transfers between devices, fsdp_permute(): return lax.ppermute(x, ('fsdp', 'ctx'), perm)  35.3 us
    ppermute x12, starting transfers between devices, tp_pair(): lax.ppermute(x, 'tp', [(i, i ^ bit) for i in range(lax.axis_size('tp'))])  16.5 us
    ppermute x11, starting transfers between devices, ctx_pair(): return lax.ppermute(x, 'ctx', [(0, 1), (1, 0)])  15.2 us
    ppermute x25, starting transfers between devices, fsdp_permute(): return lax.ppermute(x, ('fsdp', 'ctx'), perm)  12.6 us
  transfers between devices with their start and end apart: 48, of which 24 were waited for; matrix products, arithmetic and copies ran while one was open for 30% of the time, Pallas kernels for 19%

profile of v2, /device:TPU:0, one launch (start us, length us, event | category | flops | bytes accessed | tf_op | source)
XLA Modules:
  0.0 430.9 jit_solution(17597933610583090733)
XLA Ops:
  2.0 2.8 concatenate.130
  5.3 2.6 collective-permute-start.2
  8.1 3.8 constant_dynamic-slice_fusion.11
  11.9 1.9 collective-permute-start.7
  15.6 3.7 pack_attention.1
  21.8 7.3 %norm_rows.1 = bf16[2,512,2048]{2,1,0:T(8,128)(2,1)} custom-call(s32[4]{0:T(128)} %pad_add_fusion.2.order_ref, bf16[512,2048]{1,0:T(8,128)(2,1)} %bitcast.134, bf16[512,2048]{1,0:T(8,128)(2,1)} %collective-permute-done.other_ref, f32[1,2048]{1,0:T(1,128)} %bitcast.162, f32[1,2048]{1,0:T(1,128)} %bitcast.164), custom_call_target="tpu_custom_call" | custom-call | bytes 8404992 | tf_op jit(solution)/shard_map/norm_rows/pallas_call | solution.py:87
  29.1 4.2 constant_dynamic-slice_fusion.7
  42.3 4.4 %frame_rows.1 = bf16[2,512,2048]{2,1,0:T(8,128)(2,1)} custom-call(s32[4]{0:T(128)} %pad_add_fusion.2.order_ref, bf16[512,2048]{1,0:T(8,128)(2,1)} %bitcast.138, bf16[512,2048]{1,0:T(8,128)(2,1)} %collective-permute-done.4.other_ref), custom_call_target="tpu_custom_call" | custom-call | bytes 8388608 | tf_op jit(solution)/shard_map/frame_rows/pallas_call | solution.py:87
  46.7 18.1 %collective-permute-done.9.refs_7_ = bf16[512,1024]{1,0:T(8,128)(2,1)} collective-permute-done((bf16[512,1024]{1,0:T(8,128)(2,1)}, bf16[512,1024]{1,0:T(8,128)(2,1)}, u32[]{:S(2)}, u32[]{:S(2)}) %collective-permute-start.9) | collective-permute-done | bytes 1048608 | tf_op jit(solution)/shard_map/ppermute | solution.py:66
  67.1 10.9 %fusion.3 = (f32[1024,1024]{1,0:T(8,128)}, bf16[1024,1024]{1,0:T(8,128)(2,1)S(1)}) fusion(f32[1024]{0:T(1024)S(1)} %dynamic-slice_convert_fusion.4, bf16[1024,2048]{1,0:T(8,128)(2,1)} %bitcast.141, bf16[512,1024]{1,0:T(8,128)(2,1)} %collective-permute-done.9.refs_7_, bf16[512,1024]{1,0:T(8,128)(2,1)} %collective-permute-done.7.refs_6_, ...), kind=kOutput, calls=%fused_computation.4 | convolution fusion | flops 4323278848 | bytes 14684160 | tf_op jit(solution)/shard_map/dot_general | solution.py:50
  78.0 2.3 convolution_convert_fusion.4
  80.2 2.3 convolution_convert_fusion.5
  82.5 2.6 fusion.44
  85.2 2.2 convolution_convert_fusion.3
  87.4 3.1 collective-permute-done.12.refs_3_
  92.6 7.4 %project.1 = (bf16[1024,256]{1,0:T(8,128)(2,1)}, bf16[1024,512]{1,0:T(8,128)(2,1)}) custom-call(s32[1]{0:T(128)} %constant.173.clone.1._, bf16[1024,2048]{1,0:T(8,128)(2,1)} %bitcast.142, bf16[512,1024]{1,0:T(8,128)(2,1)} %get-tuple-element.103.refs_0_, bf16[512,1024]{1,0:T(8,128)(2,1)} %copy-done.4, bf16[512,1024]{1,0:T(8,128)(2,1)} %copy-done.5, ...), custom_call_target="tpu_custom_call" | custom-call | flops 3221225472 | bytes 11013120 | tf_op jit(solution)/shard_map/project/pallas_call | solution.py:87
  102.3 4.2 attended_grads.1
  108.3 9.0 %collective-permute-done.14.refs_7_ = bf16[512,1024]{1,0:T(8,128)(2,1)S(1)} collective-permute-done((bf16[512,1024]{1,0:T(8,128)(2,1)}, bf16[512,1024]{1,0:T(8,128)(2,1)S(1)}, u32[]{:S(2)}, u32[]{:S(2)}) %collective-permute-start.14) | collective-permute-done | bytes 1048608 | tf_op jit(solution)/shard_map/ppermute | solution.py:58
  117.2 8.2 %collective-permute-done.13 = bf16[2,512,512]{2,1,0:T(8,128)(2,1)S(1)} collective-permute-done((bf16[2,512,512]{2,1,0:T(8,128)(2,1)}, bf16[2,512,512]{2,1,0:T(8,128)(2,1)S(1)}, u32[]{:S(2)}, u32[]{:S(2)}) %collective-permute-start.13) | collective-permute-done | bytes 1048608 | tf_op jit(solution)/shard_map/ppermute | solution.py:66
  131.1 7.5 %share_rows.4 = bf16[512,2048]{1,0:T(8,128)(2,1)} custom-call(s32[1]{0:T(128)} %constant.173.clone.1._, bf16[1024,256]{1,0:T(8,128)(2,1)} %fusion.31.f_ref, bf16[1024,1024]{1,0:T(8,128)(2,1)} %copy-done.2, bf16[512,1024]{1,0:T(8,128)(2,1)} %get-tuple-element.103.refs_0_, bf16[512,1024]{1,0:T(8,128)(2,1)} %copy-done.4, bf16[512,1024]{1,0:T(8,128)(2,1)} %copy-done.5, ...), custom_call_target="tpu_custom_call" | custom-call | flops 2684354560 | bytes 13107200 | tf_op jit(solution)/shard_map/share_rows/pallas_call | solution.py:87
  140.3 8.9 %multiply_convert_fusion.s_ref = bf16[1024,1024]{1,0:T(8,128)(2,1)S(1)} fusion(f32[1024,1024]{1,0:T(8,128)} %get-tuple-element.198, bf16[1024,2048]{1,0:T(8,128)(2,1)} %bitcast.124, bf16[512,1024]{1,0:T(8,128)(2,1)} %copy-done.30, bf16[512,1024]{1,0:T(8,128)(2,1)} %collective-permute-done.11.refs_6_, bf16[512,1024]{1,0:T(8,128)(2,1)} %copy-done.28, ...), kind=kOutput, calls=%fused_computation.24 | convolution fusion | flops 4313841664 | bytes 14680064 | tf_op jit(solution)/shard_map/dot_general | solution.py:50
  149.2 14.0 %collective-permute-done.16 = bf16[512,1024]{1,0:T(8,128)(2,1)S(1)} collective-permute-done((bf16[512,1024]{1,0:T(8,128)(2,1)}, bf16[512,1024]{1,0:T(8,128)(2,1)S(1)}, u32[]{:S(2)}, u32[]{:S(2)}) %collective-permute-start.16) | collective-permute-done | bytes 1048608 | tf_op jit(solution)/shard_map/ppermute | solution.py:58
  172.9 7.5 %share_rows.5 = bf16[512,2048]{1,0:T(8,128)(2,1)} custom-call(s32[1]{0:T(128)} %constant.173.clone.1._, bf16[1024,256]{1,0:T(8,128)(2,1)} %fusion.31.f_ref, bf16[1024,1024]{1,0:T(8,128)(2,1)} %copy-done.2, bf16[512,1024]{1,0:T(8,128)(2,1)} %get-tuple-element.103.refs_0_, bf16[512,1024]{1,0:T(8,128)(2,1)} %copy-done.4, bf16[512,1024]{1,0:T(8,128)(2,1)} %copy-done.5, ...), custom_call_target="tpu_custom_call" | custom-call | flops 2684354560 | bytes 15204352 | tf_op jit(solution)/shard_map/share_rows/pallas_call | solution.py:87
  180.4 3.8 constant_dynamic-slice_fusion.5
  184.2 2.3 convolution_convert_fusion.2
  186.6 2.3 collective-permute-done.18
  200.7 2.2 convolution_convert_fusion.1
  206.5 3.5 convolution_convert_fusion
  210.0 4.0 fusion.39
  213.9 9.0 %collective-permute-done.20 = bf16[256,2048]{1,0:T(8,128)(2,1)} collective-permute-done((bf16[256,2048]{1,0:T(8,128)(2,1)}, bf16[256,2048]{1,0:T(8,128)(2,1)}, u32[]{:S(2)}, u32[]{:S(2)}) %collective-permute-start.20) | collective-permute-done | bytes 1048608 | tf_op jit(solution)/shard_map/ppermute | solution.py:76
  226.0 2.6 collective-permute-start.25
  229.6 2.9 add_convert_fusion.4.b_ref
  232.5 3.8 turn_back.1.f_ref
  236.3 9.2 %share_rows.6 = bf16[512,2048]{1,0:T(8,128)(2,1)} custom-call(s32[1]{0:T(128)} %constant.173.clone.1._, bf16[1024,768]{1,0:T(8,128)(2,1)} %turn_back.1.f_ref, bf16[1024,1024]{1,0:T(8,128)(2,1)} %copy-done, bf16[512,1024]{1,0:T(8,128)(2,1)} %get-tuple-element.103.refs_0_, bf16[512,1024]{1,0:T(8,128)(2,1)} %copy-done.4, bf16[512,1024]{1,0:T(8,128)(2,1)} %copy-done.5, ...), custom_call_target="tpu_custom_call" | custom-call | flops 3758096384 | bytes 14155776 | tf_op jit(solution)/shard_map/share_rows/pallas_call | solution.py:87
  245.5 2.3 convolution_convert_fusion.8
  249.0 3.3 collective-permute-done.25.got_ref
  257.3 2.4 convolution_convert_fusion.10
  261.2 3.2 finish_output.1.refs_0_
  264.4 2.3 convolution_convert_fusion.7
  268.0 3.1 collective-permute-start.27
  271.6 9.4 %share_rows.7.share_ref = bf16[512,2048]{1,0:T(8,128)(2,1)} custom-call(s32[1]{0:T(128)} %constant.173.clone.1._, bf16[1024,768]{1,0:T(8,128)(2,1)} %turn_back.1.f_ref, bf16[1024,1024]{1,0:T(8,128)(2,1)} %copy-done, bf16[512,1024]{1,0:T(8,128)(2,1)} %get-tuple-element.103.refs_0_, bf16[512,1024]{1,0:T(8,128)(2,1)} %copy-done.4, bf16[512,1024]{1,0:T(8,128)(2,1)} %copy-done.5, ...), custom_call_target="tpu_custom_call" | custom-call | flops 3758096384 | bytes 16252928 | tf_op jit(solution)/shard_map/share_rows/pallas_call | solution.py:87
  281.0 3.7 dynamic-slice_convert_fusion.1
  285.6 2.8 add_convert_fusion.3.a_ref
  288.3 2.3 convolution_convert_fusion.6
  291.7 2.7 collective-permute-done.26.refs_1_
  297.0 2.5 fusion.28
  299.5 1.9 add_convert_fusion.2.b_ref
  302.1 5.0 %norm_grads.1 = f32[2,2048]{1,0:T(2,128)} custom-call(s32[4]{0:T(128)} %pad_add_fusion.2.order_ref, bf16[512,2048]{1,0:T(8,128)(2,1)} %bitcast.136, bf16[512,2048]{1,0:T(8,128)(2,1)} %share_rows.7.share_ref), custom_call_target="tpu_custom_call" | custom-call | bytes 4210688 | tf_op jit(solution)/shard_map/norm_grads/pallas_call | solution.py:87
  307.1 3.5 fusion.32
  310.6 10.0 %collective-permute-done.36 = bf16[256,2048]{1,0:T(8,128)(2,1)} collective-permute-done((bf16[256,2048]{1,0:T(8,128)(2,1)}, bf16[256,2048]{1,0:T(8,128)(2,1)}, u32[]{:S(2)}, u32[]{:S(2)}) %collective-permute-start.36) | collective-permute-done | bytes 1048608 | tf_op jit(solution)/shard_map/ppermute | solution.py:76
  330.9 3.7 place_grad.3
  334.6 3.2 add_convert_fusion.1.a_ref
  337.9 11.6 %collective-permute-done.37.got_ref = bf16[128,2048]{1,0:T(8,128)(2,1)S(1)} collective-permute-done((bf16[128,2048]{1,0:T(8,128)(2,1)}, bf16[128,2048]{1,0:T(8,128)(2,1)S(1)}, u32[]{:S(2)}, u32[]{:S(2)}) %collective-permute-start.37) | collective-permute-done | bytes 524320 | tf_op jit(solution)/shard_map/ppermute | solution.py:76
  350.3 4.1 finish_input_grad.1.refs_0_
  354.7 2.2 collective-permute-start.28
  357.7 1.9 collective-permute-start.40
  361.7 3.7 place_grad.4
  367.4 15.7 %collective-permute-done.46.ax_ref = bf16[512,1024]{1,0:T(8,128)(2,1)S(1)} collective-permute-done((bf16[512,1024]{1,0:T(8,128)(2,1)}, bf16[512,1024]{1,0:T(8,128)(2,1)S(1)}, u32[]{:S(2)}, u32[]{:S(2)}) %collective-permute-start.46) | collective-permute-done | bytes 1048608 | tf_op jit(solution)/shard_map/ppermute | solution.py:66
  385.6 3.1 collective-permute-done.42
  392.4 13.4 %collective-permute-done.44 = f32[4864]{0:T(1024)S(1)} collective-permute-done((f32[4864]{0:T(1024)S(1)}, f32[4864]{0:T(1024)S(1)}, u32[]{:S(2)}, u32[]{:S(2)}) %collective-permute-start.44) | collective-permute-done | bytes 19488 | tf_op jit(solution)/shard_map/ppermute | solution.py:66
  406.8 3.3 gather_rows.2
  412.0 9.1 %collective-permute-done.43.refs_3_ = bf16[128,2048]{1,0:T(8,128)(2,1)} collective-permute-done((bf16[128,2048]{1,0:T(8,128)(2,1)}, bf16[128,2048]{1,0:T(8,128)(2,1)}, u32[]{:S(2)}, u32[]{:S(2)}) %collective-permute-start.43) | collective-permute-done | bytes 524320 | tf_op jit(solution)/shard_map/ppermute | solution.py:76
  421.1 4.0 gather_rows.3
  426.2 3.7 place_grad.5
  (325 shorter events, 99.8 us)
Async XLA Ops:
  4.8 14.6 %collective-permute-start.1 = (f32[2055]{0:T(1024)S(1)}, f32[2055]{0:T(1024)S(1)}, u32[]{:S(2)}, u32[]{:S(2)}) collective-permute-start(f32[2055]{0:T(1024)S(1)} %concatenate.130), channel_id=1, source_target_pairs={{0,8},{4,12},{8,0},{12,4},{16,24},{20,28},{24,16},{28,20},{1,9},{5... | collective-permute-start | bytes 24668 | tf_op jit(solution)/shard_map/ppermute | solution.py:58
  5.3 14.5 %collective-permute-start.2 = (f32[2055]{0:T(1024)S(1)}, f32[2055]{0:T(1024)S(1)}, u32[]{:S(2)}, u32[]{:S(2)}) collective-permute-start(f32[2055]{0:T(1024)S(1)} %concatenate.130), channel_id=1, source_target_pairs={{0,16},{4,28},{8,24},{12,20},{16,0},{20,12},{24,8},{28,4},{1,17},{... | collective-permute-start | bytes 24668 | tf_op jit(solution)/shard_map/ppermute | solution.py:58
  7.9 12.1 %collective-permute-start.3 = (f32[2055]{0:T(1024)S(1)}, f32[2055]{0:T(1024)S(1)}, u32[]{:S(2)}, u32[]{:S(2)}) collective-permute-start(f32[2055]{0:T(1024)S(1)} %concatenate.130), channel_id=1, source_target_pairs={{0,24},{4,20},{8,16},{12,28},{16,8},{20,4},{24,0},{28,12},{1,25},{... | collective-permute-start | bytes 24668 | tf_op jit(solution)/shard_map/ppermute | solution.py:58
  7.9 12.1 %collective-permute-start = (bf16[512,2048]{1,0:T(8,128)(2,1)}, bf16[512,2048]{1,0:T(8,128)(2,1)}, u32[]{:S(2)}, u32[]{:S(2)}) collective-permute-start(bf16[512,2048]{1,0:T(8,128)(2,1)} %bitcast.133), channel_id=1, source_target_pairs={{0,8},{4,12},{8,0},{12,4},{16,24},{20,28},{24,16},{28,20},{1,9},{5... | collective-permute-start | bytes 6291464 | tf_op jit(solution)/shard_map/ppermute | solution.py:58
  11.9 26.9 %collective-permute-start.7 = (bf16[512,1024]{1,0:T(8,128)(2,1)}, bf16[512,1024]{1,0:T(8,128)(2,1)}, u32[]{:S(2)}, u32[]{:S(2)}) collective-permute-start(bf16[512,1024]{1,0:T(8,128)(2,1)} %get-tuple-element.208), channel_id=1, source_target_pairs={{0,16},{4,28},{8,24},{12,20},{16,0},{20,12},{24,8},{28,4},{1,17},{... | collective-permute-start | bytes 3145736 | tf_op jit(solution)/shard_map/ppermute | solution.py:58
  20.0 18.8 %collective-permute-start.4 = (bf16[512,2048]{1,0:T(8,128)(2,1)S(1)}, bf16[512,2048]{1,0:T(8,128)(2,1)}, u32[]{:S(2)}, u32[]{:S(2)}) collective-permute-start(bf16[512,2048]{1,0:T(8,128)(2,1)S(1)} %bitcast.140), channel_id=1, source_target_pairs={{0,8},{4,12},{8,0},{12,4},{16,24},{20,28},{24,16},{28,20},{1,9},{5... | collective-permute-start | bytes 6291464 | tf_op jit(solution)/shard_map/ppermute | solution.py:58
  21.3 17.5 %collective-permute-start.6 = (bf16[512,1024]{1,0:T(8,128)(2,1)}, bf16[512,1024]{1,0:T(8,128)(2,1)S(1)}, u32[]{:S(2)}, u32[]{:S(2)}) collective-permute-start(bf16[512,1024]{1,0:T(8,128)(2,1)} %get-tuple-element.111), channel_id=1, source_target_pairs={{0,8},{4,12},{8,0},{12,4},{16,24},{20,28},{24,16},{28,20},{1,9},{5... | collective-permute-start | bytes 3145736 | tf_op jit(solution)/shard_map/ppermute | solution.py:58
  21.8 17.0 %collective-permute-start.5 = (bf16[512,1024]{1,0:T(8,128)(2,1)}, bf16[512,1024]{1,0:T(8,128)(2,1)}, u32[]{:S(2)}, u32[]{:S(2)}) collective-permute-start(bf16[512,1024]{1,0:T(8,128)(2,1)} %get-tuple-element.110), channel_id=1, source_target_pairs={{0,8},{4,12},{8,0},{12,4},{16,24},{20,28},{24,16},{28,20},{1,9},{5... | collective-permute-start | bytes 3145736 | tf_op jit(solution)/shard_map/ppermute | solution.py:58
  38.8 7.9 %collective-permute-start.10 = (bf16[512,1024]{1,0:T(8,128)(2,1)}, bf16[512,1024]{1,0:T(8,128)(2,1)S(1)}, u32[]{:S(2)}, u32[]{:S(2)}) collective-permute-start(bf16[512,1024]{1,0:T(8,128)(2,1)} %get-tuple-element.115), channel_id=1, source_target_pairs={{0,8},{4,12},{8,0},{12,4},{16,24},{20,28},{24,16},{28,20},{1,9},{5... | collective-permute-start | bytes 3145736 | tf_op jit(solution)/shard_map/ppermute | solution.py:58
  39.4 25.5 %collective-permute-start.9 = (bf16[512,1024]{1,0:T(8,128)(2,1)}, bf16[512,1024]{1,0:T(8,128)(2,1)}, u32[]{:S(2)}, u32[]{:S(2)}) collective-permute-start(bf16[512,1024]{1,0:T(8,128)(2,1)} %collective-permute-done.7.refs_6_), channel_id=1, source_target_pairs={{0,4},{4,0},{1,5},{5,1},{2,6},{6,2},{3,7},{7,3},{8,12},{12,8},{9,1... | collective-permute-start | bytes 3145736 | tf_op jit(solution)/shard_map/ppermute | solution.py:66
  40.9 25.1 %collective-permute-start.8 = (bf16[512,1024]{1,0:T(8,128)(2,1)}, bf16[512,1024]{1,0:T(8,128)(2,1)S(1)}, u32[]{:S(2)}, u32[]{:S(2)}) collective-permute-start(bf16[512,1024]{1,0:T(8,128)(2,1)} %get-tuple-element.113), channel_id=1, source_target_pairs={{0,16},{4,28},{8,24},{12,20},{16,0},{20,12},{24,8},{28,4},{1,17},{... | collective-permute-start | bytes 3145736 | tf_op jit(solution)/shard_map/ppermute | solution.py:58
  46.7 19.2 %copy-start.28 = (bf16[512,1024]{1,0:T(8,128)(2,1)}, bf16[512,1024]{1,0:T(8,128)(2,1)S(1)}, u32[]{:S(2)}) copy-start(bf16[512,1024]{1,0:T(8,128)(2,1)S(1)} %collective-permute-done.10.refs_5_) | copy-start | bytes 3145732
  66.0 24.5 %collective-permute-start.12 = (bf16[512,1024]{1,0:T(8,128)(2,1)S(1)}, bf16[512,1024]{1,0:T(8,128)(2,1)S(1)}, u32[]{:S(2)}, u32[]{:S(2)}) collective-permute-start(bf16[512,1024]{1,0:T(8,128)(2,1)S(1)} %collective-permute-done.8.refs_2_), channel_id=1, source_target_pairs={{0,4},{4,0},{1,5},{5,1},{2,6},{6,2},{3,7},{7,3},{8,12},{12,8},{9,1... | collective-permute-start | bytes 3145736 | tf_op jit(solution)/shard_map/ppermute | solution.py:66
  67.1 25.2 %collective-permute-start.11 = (bf16[512,1024]{1,0:T(8,128)(2,1)}, bf16[512,1024]{1,0:T(8,128)(2,1)}, u32[]{:S(2)}, u32[]{:S(2)}) collective-permute-start(bf16[512,1024]{1,0:T(8,128)(2,1)} %get-tuple-element.118), channel_id=1, source_target_pairs={{0,16},{4,28},{8,24},{12,20},{16,0},{20,12},{24,8},{28,4},{1,17},{... | collective-permute-start | bytes 3145736 | tf_op jit(solution)/shard_map/ppermute | solution.py:58
  92.2 16.0 %collective-permute-start.15 = (bf16[512,1024]{1,0:T(8,128)(2,1)}, bf16[512,1024]{1,0:T(8,128)(2,1)}, u32[]{:S(2)}, u32[]{:S(2)}) collective-permute-start(bf16[512,1024]{1,0:T(8,128)(2,1)} %convolution_convert_fusion.3), channel_id=1, source_target_pairs={{0,8},{4,12},{8,0},{12,4},{16,24},{20,28},{24,16},{28,20},{1,9},{5... | collective-permute-start | bytes 3145736 | tf_op jit(solution)/shard_map/ppermute | solution.py:58
  92.3 25.0 %collective-permute-start.14 = (bf16[512,1024]{1,0:T(8,128)(2,1)}, bf16[512,1024]{1,0:T(8,128)(2,1)S(1)}, u32[]{:S(2)}, u32[]{:S(2)}) collective-permute-start(bf16[512,1024]{1,0:T(8,128)(2,1)} %get-tuple-element.124), channel_id=1, source_target_pairs={{0,24},{4,20},{8,16},{12,28},{16,8},{20,4},{24,0},{28,12},{1,25},{... | collective-permute-start | bytes 3145736 | tf_op jit(solution)/shard_map/ppermute | solution.py:58
  100.0 25.4 %collective-permute-start.13 = (bf16[2,512,512]{2,1,0:T(8,128)(2,1)}, bf16[2,512,512]{2,1,0:T(8,128)(2,1)S(1)}, u32[]{:S(2)}, u32[]{:S(2)}) collective-permute-start(bf16[2,512,512]{2,1,0:T(8,128)(2,1)} %bitcast.151), channel_id=1, source_target_pairs={{0,4},{4,0},{1,5},{5,1},{2,6},{6,2},{3,7},{7,3},{8,12},{12,8},{9,1... | collective-permute-start | bytes 3145736 | tf_op jit(solution)/shard_map/ppermute | solution.py:66
  102.3 23.2 %copy-start.13 = (bf16[1024,512]{1,0:T(8,128)(2,1)S(1)}, bf16[1024,512]{1,0:T(8,128)(2,1)}, u32[]{:S(2)}) copy-start(bf16[1024,512]{1,0:T(8,128)(2,1)} %get-tuple-element.122) | copy-start | bytes 3145732
  106.4 19.0 %copy-start.55 = (bf16[1024,256]{1,0:T(8,128)(2,1)S(1)}, bf16[1024,256]{1,0:T(8,128)(2,1)}, u32[]{:S(2)}) copy-start(bf16[1024,256]{1,0:T(8,128)(2,1)} %get-tuple-element.121) | copy-start | bytes 1572868
  138.6 24.6 %copy-start.31 = (bf16[512,2048]{1,0:T(8,128)(2,1)S(1)}, bf16[512,2048]{1,0:T(8,128)(2,1)}, u32[]{:S(2)}) copy-start(bf16[512,2048]{1,0:T(8,128)(2,1)} %share_rows.4) | copy-start | bytes 6291460
  138.6 26.2 %copy-start.20 = (f32[512,1024]{1,0:T(8,128)S(1)}, f32[512,1024]{1,0:T(8,128)}, u32[]{:S(2)}) copy-start(f32[512,1024]{1,0:T(8,128)} %fusion.44) | copy-start | bytes 6291460
  138.6 24.6 %collective-permute-start.16 = (bf16[512,1024]{1,0:T(8,128)(2,1)}, bf16[512,1024]{1,0:T(8,128)(2,1)S(1)}, u32[]{:S(2)}, u32[]{:S(2)}) collective-permute-start(bf16[512,1024]{1,0:T(8,128)(2,1)} %convolution_convert_fusion.5), channel_id=1, source_target_pairs={{0,16},{4,20},{8,24},{12,28},{16,0},{20,4},{24,8},{28,12},{1,17},{... | collective-permute-start | bytes 3145736 | tf_op jit(solution)/shard_map/ppermute | solution.py:58
  140.3 27.2 %copy-start.42 = (bf16[512,256]{1,0:T(8,128)(2,1)S(1)}, bf16[512,256]{1,0:T(8,128)(2,1)}, u32[]{:S(2)}) copy-start(bf16[512,256]{1,0:T(8,128)(2,1)} %get-tuple-element.130) | copy-start | bytes 786436
  149.2 60.8 %copy-start = (bf16[1024,1024]{1,0:T(8,128)(2,1)}, bf16[1024,1024]{1,0:T(8,128)(2,1)S(1)}, u32[]{:S(2)}) copy-start(bf16[1024,1024]{1,0:T(8,128)(2,1)S(1)} %multiply_convert_fusion.s_ref) | copy-start | bytes 6291460
  149.2 18.3 %copy-start.14 = (bf16[1024,512]{1,0:T(8,128)(2,1)S(1)}, bf16[1024,512]{1,0:T(8,128)(2,1)}, u32[]{:S(2)}) copy-start(bf16[1024,512]{1,0:T(8,128)(2,1)} %get-tuple-element.122) | copy-start | bytes 3145732
  149.2 18.3 %copy-start.16 = (bf16[2,512,512]{2,1,0:T(8,128)(2,1)S(1)}, bf16[2,512,512]{2,1,0:T(8,128)(2,1)}, u32[]{:S(2)}) copy-start(bf16[2,512,512]{2,1,0:T(8,128)(2,1)} %copy-done.15) | copy-start | bytes 3145732
  149.2 18.3 %copy-start.25 = (f32[512,1024]{1,0:T(8,128)S(1)}, f32[512,1024]{1,0:T(8,128)}, u32[]{:S(2)}) copy-start(f32[512,1024]{1,0:T(8,128)} %copy-done.24) | copy-start | bytes 6291460
  163.2 25.7 %collective-permute-start.18 = (bf16[512,1024]{1,0:T(8,128)(2,1)}, bf16[512,1024]{1,0:T(8,128)(2,1)}, u32[]{:S(2)}, u32[]{:S(2)}) collective-permute-start(bf16[512,1024]{1,0:T(8,128)(2,1)} %convolution_convert_fusion.4), channel_id=1, source_target_pairs={{0,24},{4,28},{8,16},{12,20},{16,8},{20,12},{24,0},{28,4},{1,25},{... | collective-permute-start | bytes 3145736 | tf_op jit(solution)/shard_map/ppermute | solution.py:58
  163.2 9.7 %collective-permute-start.17 = (bf16[512,2048]{1,0:T(8,128)(2,1)S(1)}, bf16[512,2048]{1,0:T(8,128)(2,1)}, u32[]{:S(2)}, u32[]{:S(2)}) collective-permute-start(bf16[512,2048]{1,0:T(8,128)(2,1)S(1)} %copy-done.31), channel_id=1, source_target_pairs={{0,8},{4,12},{8,0},{12,4},{16,24},{20,28},{24,16},{28,20},{1,9},{5... | collective-permute-start | bytes 6291464 | tf_op jit(solution)/shard_map/ppermute | solution.py:58
  166.2 47.7 %collective-permute-start.21 = (bf16[512,1024]{1,0:T(8,128)(2,1)}, bf16[512,1024]{1,0:T(8,128)(2,1)}, u32[]{:S(2)}, u32[]{:S(2)}) collective-permute-start(bf16[512,1024]{1,0:T(8,128)(2,1)} %add_convert_fusion.5.a_ref), channel_id=1, source_target_pairs={{0,4},{4,0},{1,5},{5,1},{2,6},{6,2},{3,7},{7,3},{8,12},{12,8},{9,1... | collective-permute-start | bytes 3145736 | tf_op jit(solution)/shard_map/ppermute | solution.py:66
  197.4 25.5 %collective-permute-start.20 = (bf16[256,2048]{1,0:T(8,128)(2,1)}, bf16[256,2048]{1,0:T(8,128)(2,1)}, u32[]{:S(2)}, u32[]{:S(2)}) collective-permute-start(bf16[256,2048]{1,0:T(8,128)(2,1)} %get-tuple-element.139), channel_id=1, source_target_pairs={{0,1},{1,0},{2,3},{3,2},{4,5},{5,4},{6,7},{7,6},{8,9},{9,8},{10,11... | collective-permute-start | bytes 3145736 | tf_op jit(solution)/shard_map/ppermute | solution.py:76
  199.0 25.3 %collective-permute-start.19 = (bf16[512,1024]{1,0:T(8,128)(2,1)}, bf16[512,1024]{1,0:T(8,128)(2,1)}, u32[]{:S(2)}, u32[]{:S(2)}) collective-permute-start(bf16[512,1024]{1,0:T(8,128)(2,1)} %convolution_convert_fusion.2), channel_id=1, source_target_pairs={{0,16},{4,20},{8,24},{12,28},{16,0},{20,4},{24,8},{28,12},{1,17},{... | collective-permute-start | bytes 3145736 | tf_op jit(solution)/shard_map/ppermute | solution.py:58
  202.9 21.3 %collective-permute-start.22 = (bf16[512,1024]{1,0:T(8,128)(2,1)}, bf16[512,1024]{1,0:T(8,128)(2,1)}, u32[]{:S(2)}, u32[]{:S(2)}) collective-permute-start(bf16[512,1024]{1,0:T(8,128)(2,1)} %convolution_convert_fusion.1), channel_id=1, source_target_pairs={{0,8},{4,12},{8,0},{12,4},{16,24},{20,28},{24,16},{28,20},{1,9},{5... | collective-permute-start | bytes 3145736 | tf_op jit(solution)/shard_map/ppermute | solution.py:58
  204.8 27.8 %collective-permute-start.23 = (bf16[2,512,512]{2,1,0:T(8,128)(2,1)S(1)}, bf16[2,512,512]{2,1,0:T(8,128)(2,1)}, u32[]{:S(2)}, u32[]{:S(2)}) collective-permute-start(bf16[2,512,512]{2,1,0:T(8,128)(2,1)S(1)} %copy-done.36), channel_id=1, source_target_pairs={{0,4},{4,0},{1,5},{5,1},{2,6},{6,2},{3,7},{7,3},{8,12},{12,8},{9,1... | collective-permute-start | bytes 3145736 | tf_op jit(solution)/shard_map/ppermute | solution.py:66
  210.0 14.3 %copy-start.19 = (f32[256,2048]{1,0:T(8,128)S(1)}, f32[256,2048]{1,0:T(8,128)}, u32[]{:S(2)}) copy-start(f32[256,2048]{1,0:T(8,128)} %get-tuple-element.140) | copy-start | bytes 6291460
  224.3 28.0 %collective-permute-start.24 = (bf16[512,1024]{1,0:T(8,128)(2,1)}, bf16[512,1024]{1,0:T(8,128)(2,1)}, u32[]{:S(2)}, u32[]{:S(2)}) collective-permute-start(bf16[512,1024]{1,0:T(8,128)(2,1)} %convolution_convert_fusion), channel_id=1, source_target_pairs={{0,24},{4,28},{8,16},{12,20},{16,8},{20,12},{24,0},{28,4},{1,25},{... | collective-permute-start | bytes 3145736 | tf_op jit(solution)/shard_map/ppermute | solution.py:58
  226.0 26.3 %collective-permute-start.25 = (bf16[128,2048]{1,0:T(8,128)(2,1)S(1)}, bf16[128,2048]{1,0:T(8,128)(2,1)S(1)}, u32[]{:S(2)}, u32[]{:S(2)}) collective-permute-start(bf16[128,2048]{1,0:T(8,128)(2,1)S(1)} %dynamic-slice_convert_fusion.2), channel_id=1, source_target_pairs={{0,2},{1,3},{2,0},{3,1},{4,6},{5,7},{6,4},{7,5},{8,10},{9,11},{10,... | collective-permute-start | bytes 1572872 | tf_op jit(solution)/shard_map/ppermute | solution.py:76
  252.3 18.9 %collective-permute-start.31 = (bf16[512,2048]{1,0:T(8,128)(2,1)}, bf16[512,2048]{1,0:T(8,128)(2,1)}, u32[]{:S(2)}, u32[]{:S(2)}) collective-permute-start(bf16[512,2048]{1,0:T(8,128)(2,1)} %share_rows.6), channel_id=1, source_target_pairs={{0,8},{4,12},{8,0},{12,4},{16,24},{20,28},{24,16},{28,20},{1,9},{5... | collective-permute-start | bytes 6291464 | tf_op jit(solution)/shard_map/ppermute | solution.py:58
  259.7 25.8 %collective-permute-start.30 = (bf16[512,1024]{1,0:T(8,128)(2,1)}, bf16[512,1024]{1,0:T(8,128)(2,1)}, u32[]{:S(2)}, u32[]{:S(2)}) collective-permute-start(bf16[512,1024]{1,0:T(8,128)(2,1)} %add_convert_fusion.4.b_ref), channel_id=1, source_target_pairs={{0,4},{4,0},{1,5},{5,1},{2,6},{6,2},{3,7},{7,3},{8,12},{12,8},{9,1... | collective-permute-start | bytes 3145736 | tf_op jit(solution)/shard_map/ppermute | solution.py:66
  267.9 28.4 %collective-permute-start.29 = (bf16[512,1024]{1,0:T(8,128)(2,1)}, bf16[512,1024]{1,0:T(8,128)(2,1)}, u32[]{:S(2)}, u32[]{:S(2)}) collective-permute-start(bf16[512,1024]{1,0:T(8,128)(2,1)} %pad_maximum_fusion.5), channel_id=1, source_target_pairs={{0,8},{4,12},{8,0},{12,4},{16,24},{20,28},{24,16},{28,20},{1,9},{5... | collective-permute-start | bytes 3145736 | tf_op jit(solution)/shard_map/ppermute | solution.py:58
  268.0 26.4 %collective-permute-start.26 = (bf16[128,2048]{1,0:T(8,128)(2,1)S(1)}, bf16[128,2048]{1,0:T(8,128)(2,1)}, u32[]{:S(2)}, u32[]{:S(2)}) collective-permute-start(bf16[128,2048]{1,0:T(8,128)(2,1)S(1)} %copy-done.32), channel_id=1, source_target_pairs={{0,2},{1,3},{2,0},{3,1},{4,6},{5,7},{6,4},{7,5},{8,10},{9,11},{10,... | collective-permute-start | bytes 1572872 | tf_op jit(solution)/shard_map/ppermute | solution.py:76
  268.0 26.5 %collective-permute-start.27 = (bf16[128,2048]{1,0:T(8,128)(2,1)S(1)}, bf16[128,2048]{1,0:T(8,128)(2,1)S(1)}, u32[]{:S(2)}, u32[]{:S(2)}) collective-permute-start(bf16[128,2048]{1,0:T(8,128)(2,1)S(1)} %copy-done.32), channel_id=1, source_target_pairs={{0,1},{1,0},{2,3},{3,2},{4,5},{5,4},{6,7},{7,6},{8,9},{9,8},{10,11... | collective-permute-start | bytes 1572872 | tf_op jit(solution)/shard_map/ppermute | solution.py:76
  271.1 25.2 %collective-permute-start.32 = (bf16[512,1024]{1,0:T(8,128)(2,1)}, bf16[512,1024]{1,0:T(8,128)(2,1)}, u32[]{:S(2)}, u32[]{:S(2)}) collective-permute-start(bf16[512,1024]{1,0:T(8,128)(2,1)} %pad_maximum_fusion.4), channel_id=1, source_target_pairs={{0,16},{4,20},{8,24},{12,28},{16,0},{20,4},{24,8},{28,12},{1,17},{... | collective-permute-start | bytes 3145736 | tf_op jit(solution)/shard_map/ppermute | solution.py:58
  296.3 24.3 %collective-permute-start.36 = (bf16[256,2048]{1,0:T(8,128)(2,1)}, bf16[256,2048]{1,0:T(8,128)(2,1)}, u32[]{:S(2)}, u32[]{:S(2)}) collective-permute-start(bf16[256,2048]{1,0:T(8,128)(2,1)} %get-tuple-element.154), channel_id=1, source_target_pairs={{0,1},{1,0},{2,3},{3,2},{4,5},{5,4},{6,7},{7,6},{8,9},{9,8},{10,11... | collective-permute-start | bytes 3145736 | tf_op jit(solution)/shard_map/ppermute | solution.py:76
  296.6 25.0 %collective-permute-start.33 = (bf16[512,1024]{1,0:T(8,128)(2,1)}, bf16[512,1024]{1,0:T(8,128)(2,1)}, u32[]{:S(2)}, u32[]{:S(2)}) collective-permute-start(bf16[512,1024]{1,0:T(8,128)(2,1)} %pad_maximum_fusion.6), channel_id=1, source_target_pairs={{0,24},{4,28},{8,16},{12,20},{16,8},{20,12},{24,0},{28,4},{1,25},{... | collective-permute-start | bytes 3145736 | tf_op jit(solution)/shard_map/ppermute | solution.py:58
  301.4 26.2 %copy-start.29 = (bf16[512,1024]{1,0:T(8,128)(2,1)}, bf16[512,1024]{1,0:T(8,128)(2,1)S(1)}, u32[]{:S(2)}) copy-start(bf16[512,1024]{1,0:T(8,128)(2,1)S(1)} %add_convert_fusion.2.b_ref) | copy-start | bytes 3145732
  301.4 26.2 %collective-permute-start.34 = (bf16[512,1024]{1,0:T(8,128)(2,1)}, bf16[512,1024]{1,0:T(8,128)(2,1)}, u32[]{:S(2)}, u32[]{:S(2)}) collective-permute-start(bf16[512,1024]{1,0:T(8,128)(2,1)} %add_convert_fusion.3.a_ref), channel_id=1, source_target_pairs={{0,4},{4,0},{1,5},{5,1},{2,6},{6,2},{3,7},{7,3},{8,12},{12,8},{9,1... | collective-permute-start | bytes 3145736 | tf_op jit(solution)/shard_map/ppermute | solution.py:66
  307.0 14.5 %copy-start.23 = (f32[256,2048]{1,0:T(8,128)S(1)}, f32[256,2048]{1,0:T(8,128)}, u32[]{:S(2)}) copy-start(f32[256,2048]{1,0:T(8,128)} %get-tuple-element.155) | copy-start | bytes 6291460
  324.0 25.5 %collective-permute-start.37 = (bf16[128,2048]{1,0:T(8,128)(2,1)}, bf16[128,2048]{1,0:T(8,128)(2,1)S(1)}, u32[]{:S(2)}, u32[]{:S(2)}) collective-permute-start(bf16[128,2048]{1,0:T(8,128)(2,1)} %dynamic-slice_convert_fusion), channel_id=1, source_target_pairs={{0,2},{1,3},{2,0},{3,1},{4,6},{5,7},{6,4},{7,5},{8,10},{9,11},{10,... | collective-permute-start | bytes 1572872 | tf_op jit(solution)/shard_map/ppermute | solution.py:76
  327.6 32.1 %collective-permute-start.35 = (bf16[512,1024]{1,0:T(8,128)(2,1)S(1)}, bf16[512,1024]{1,0:T(8,128)(2,1)}, u32[]{:S(2)}, u32[]{:S(2)}) collective-permute-start(bf16[512,1024]{1,0:T(8,128)(2,1)S(1)} %add_convert_fusion.2.b_ref), channel_id=1, source_target_pairs={{0,4},{4,0},{1,5},{5,1},{2,6},{6,2},{3,7},{7,3},{8,12},{12,8},{9,1... | collective-permute-start | bytes 3145736 | tf_op jit(solution)/shard_map/ppermute | solution.py:66
  329.1 8.7 %collective-permute-start.38 = (f32[2,2048]{1,0:T(2,128)S(1)}, f32[2,2048]{1,0:T(2,128)S(1)}, u32[]{:S(2)}, u32[]{:S(2)}) collective-permute-start(f32[2,2048]{1,0:T(2,128)S(1)} %copy-done.44), channel_id=1, source_target_pairs={{0,1},{1,0},{2,3},{3,2},{4,5},{5,4},{6,7},{7,6},{8,9},{9,8},{10,11... | collective-permute-start | bytes 49160 | tf_op jit(solution)/shard_map/ppermute | solution.py:76
  354.4 5.3 %collective-permute-start.41 = (f32[2,2048]{1,0:T(2,128)S(1)}, f32[2,2048]{1,0:T(2,128)S(1)}, u32[]{:S(2)}, u32[]{:S(2)}) collective-permute-start(f32[2,2048]{1,0:T(2,128)S(1)} %add.365), channel_id=1, source_target_pairs={{0,2},{1,3},{2,0},{3,1},{4,6},{5,7},{6,4},{7,5},{8,10},{9,11},{10,... | collective-permute-start | bytes 49160 | tf_op jit(solution)/shard_map/ppermute | solution.py:76
  354.7 51.8 %collective-permute-start.28 = (bf16[128,2048]{1,0:T(8,128)(2,1)}, bf16[128,2048]{1,0:T(8,128)(2,1)}, u32[]{:S(2)}, u32[]{:S(2)}) collective-permute-start(bf16[128,2048]{1,0:T(8,128)(2,1)} %collective-permute-done.26.refs_1_), channel_id=1, source_target_pairs={{0,1},{1,0},{2,3},{3,2},{4,5},{5,4},{6,7},{7,6},{8,9},{9,8},{10,11... | collective-permute-start | bytes 1572872 | tf_op jit(solution)/shard_map/ppermute | solution.py:76
  356.9 31.9 %collective-permute-start.39 = (bf16[128,2048]{1,0:T(8,128)(2,1)}, bf16[128,2048]{1,0:T(8,128)(2,1)}, u32[]{:S(2)}, u32[]{:S(2)}) collective-permute-start(bf16[128,2048]{1,0:T(8,128)(2,1)} %finish_input_grad.1.refs_0_), channel_id=1, source_target_pairs={{0,2},{1,3},{2,0},{3,1},{4,6},{5,7},{6,4},{7,5},{8,10},{9,11},{10,... | collective-permute-start | bytes 1572872 | tf_op jit(solution)/shard_map/ppermute | solution.py:76
  357.7 32.8 %collective-permute-start.40 = (bf16[128,2048]{1,0:T(8,128)(2,1)}, bf16[128,2048]{1,0:T(8,128)(2,1)}, u32[]{:S(2)}, u32[]{:S(2)}) collective-permute-start(bf16[128,2048]{1,0:T(8,128)(2,1)} %finish_input_grad.1.refs_0_), channel_id=1, source_target_pairs={{0,1},{1,0},{2,3},{3,2},{4,5},{5,4},{6,7},{7,6},{8,9},{9,8},{10,11... | collective-permute-start | bytes 1572872 | tf_op jit(solution)/shard_map/ppermute | solution.py:76
  359.7 23.4 %collective-permute-start.46 = (bf16[512,1024]{1,0:T(8,128)(2,1)}, bf16[512,1024]{1,0:T(8,128)(2,1)S(1)}, u32[]{:S(2)}, u32[]{:S(2)}) collective-permute-start(bf16[512,1024]{1,0:T(8,128)(2,1)} %add_convert_fusion.1.a_ref), channel_id=1, source_target_pairs={{0,4},{4,0},{1,5},{5,1},{2,6},{6,2},{3,7},{7,3},{8,12},{12,8},{9,1... | collective-permute-start | bytes 3145736 | tf_op jit(solution)/shard_map/ppermute | solution.py:66
  367.4 42.7 %copy-start.27 = (bf16[512,1024]{1,0:T(8,128)(2,1)}, bf16[512,1024]{1,0:T(8,128)(2,1)S(1)}, u32[]{:S(2)}) copy-start(bf16[512,1024]{1,0:T(8,128)(2,1)S(1)} %add_convert_fusion.b_ref) | copy-start | bytes 3145732
  383.2 26.9 %copy-start.34 = (bf16[512,1024]{1,0:T(8,128)(2,1)}, bf16[512,1024]{1,0:T(8,128)(2,1)S(1)}, u32[]{:S(2)}) copy-start(bf16[512,1024]{1,0:T(8,128)(2,1)S(1)} %collective-permute-done.46.ax_ref) | copy-start | bytes 3145732
  383.2 42.0 %collective-permute-start.47 = (bf16[512,1024]{1,0:T(8,128)(2,1)S(1)}, bf16[512,1024]{1,0:T(8,128)(2,1)S(1)}, u32[]{:S(2)}, u32[]{:S(2)}) collective-permute-start(bf16[512,1024]{1,0:T(8,128)(2,1)S(1)} %add_convert_fusion.b_ref), channel_id=1, source_target_pairs={{0,4},{4,0},{1,5},{5,1},{2,6},{6,2},{3,7},{7,3},{8,12},{12,8},{9,1... | collective-permute-start | bytes 3145736 | tf_op jit(solution)/shard_map/ppermute | solution.py:66
  384.9 3.8 collective-permute-start.42
  390.5 15.3 %collective-permute-start.44 = (f32[4864]{0:T(1024)S(1)}, f32[4864]{0:T(1024)S(1)}, u32[]{:S(2)}, u32[]{:S(2)}) collective-permute-start(f32[4864]{0:T(1024)S(1)} %add.376), channel_id=1, source_target_pairs={{0,4},{4,0},{1,5},{5,1},{2,6},{6,2},{3,7},{7,3},{8,12},{12,8},{9,1... | collective-permute-start | bytes 58376 | tf_op jit(solution)/shard_map/ppermute | solution.py:66
  405.8 4.3 %collective-permute-start.45 = (f32[3328]{0:T(1024)S(1)}, f32[3328]{0:T(1024)S(1)}, u32[]{:S(2)}, u32[]{:S(2)}) collective-permute-start(f32[3328]{0:T(1024)S(1)} %slice.223), channel_id=1, source_target_pairs={{0,8},{4,12},{8,0},{12,4},{16,24},{20,28},{24,16},{28,20},{1,9},{5... | collective-permute-start | bytes 39944 | tf_op jit(solution)/shard_map/ppermute | solution.py:58
  406.5 14.6 %collective-permute-start.43 = (bf16[128,2048]{1,0:T(8,128)(2,1)}, bf16[128,2048]{1,0:T(8,128)(2,1)}, u32[]{:S(2)}, u32[]{:S(2)}) collective-permute-start(bf16[128,2048]{1,0:T(8,128)(2,1)} %collective-permute-done.39.refs_1_), channel_id=1, source_target_pairs={{0,1},{1,0},{2,3},{3,2},{4,5},{5,4},{6,7},{7,6},{8,9},{9,8},{10,11... | collective-permute-start | bytes 1572872 | tf_op jit(solution)/shard_map/ppermute | solution.py:76
  410.8 19.1 %copy-start.46 = (f32[512]{0:T(512)}, f32[512]{0:T(512)S(1)}, u32[]{:S(2)}) copy-start(f32[512]{0:T(512)S(1)} %get-tuple-element.286) | copy-start | bytes 6148
  (42 other events, 188.3 us)
